TPU v7x, 128 devices: a whole 4x4x4 slice. The times are simulated.
128 devices in a mesh: gx: 8 (over x_lo, y), gy: 16 (over z, x_hi, core).
Axes of the slice: x: 4 (x_hi: 2, x_lo: 2; x = x_hi * 2 + x_lo), y: 4, z: 4, core: 2. Of those that a mesh axis runs over, the one named last changes fastest.
Arguments:
- features: bfloat16 [256, 512, 128], P(('gx', 'gy')), may hold values from -11 to 11
- brick_pos: int32 [256], P(('gx', 'gy')), may hold values from 0 to 4, as said below
- cotangent: bfloat16 [256, 512, 128], P(('gx', 'gy')), may hold values from -40 to 40
- first_kernel: bfloat16 [27, 128, 128], replicated, may hold values from -0.109375 to 0.109375
- second_kernel: bfloat16 [27, 128, 128], replicated, may hold values from -0.109375 to 0.109375
- norm_gain: float32 [128], replicated, may hold values from 0.1 to 1.9
Outputs:
- block_out: bfloat16 [256, 512, 128], P(('gx', 'gy'))
- feature_grad: bfloat16 [256, 512, 128], P(('gx', 'gy'))
- kernel_update: float32 [2, 27, 128, 128], replicated
- gain_update: float32 [128], replicated
Inputs may be any that keep to these rules, and one draw needn't show every extreme that they name: `brick_pos`: on each device block the first k slots (k between max(1, 0) and 2, and k = 2 on at least one block) hold distinct positions below 4; the remaining slots hold 4.
All inputs are finite; a program needn't handle non-finite values.
Results may differ from a plain program's by a relative error of at most 0.0029.
Values may be sent and summed in bfloat16 or wider, within the bound.
A program may use at most 128 MiB of HBM per device.

v0:
```python
import jax
import jax.numpy as jnp
from jax import lax
from jax.sharding import PartitionSpec as P

BX = 2
BY = 2
BZ = 1
POS = 4


clip_level = 0.5


def with_halo(cells, sides, width):
    for axis, dim in sides:
        count = lax.axis_size(axis)
        ends = count - 1
        head = lax.slice_in_dim(cells, 0, width, axis=dim)
        tail = lax.slice_in_dim(cells, cells.shape[dim] - width, cells.shape[dim], axis=dim)
        cells = jnp.concatenate(
            [
                lax.ppermute(tail, axis, [(i, (i + 1) % count) for i in range(ends)]),
                cells,
                lax.ppermute(head, axis, [((i + 1) % count, i) for i in range(ends)]),
            ],
            axis=dim,
        )
    return cells


def brick_coords(position):
    brick_x = position // (BY * BZ)
    brick_y = position // BZ % BY
    brick_z = position % BZ
    return (brick_x, brick_y, brick_z)


def activate(pre, norm_gain):
    average = jnp.mean(pre, axis=-1, keepdims=True)
    center = pre - average
    spread = jnp.mean(center * center, axis=-1, keepdims=True)
    normed = center * lax.rsqrt(spread + 1e-05) * norm_gain
    return normed * jax.nn.sigmoid(normed)


def apply_taps(tile_set, kernel, flipped):
    slot_count, channels = (tile_set.shape[0], tile_set.shape[-1])
    summed = jnp.zeros((slot_count * 512, channels), jnp.float32)
    for step_x in range(3):
        for step_y in range(3):
            for step_z in range(3):
                tap_index = (step_x * 3 + step_y) * 3 + step_z
                if flipped:
                    start_x, start_y, start_z = (2 - step_x, 2 - step_y, 2 - step_z)
                else:
                    start_x, start_y, start_z = (step_x, step_y, step_z)
                window = tile_set[
                    :, start_x : start_x + 8, start_y : start_y + 8, start_z : start_z + 8, :
                ]
                window = window.reshape(slot_count * 512, channels)
                if flipped:
                    summed = summed + lax.dot_general(
                        window,
                        kernel[tap_index],
                        (((1,), (1,)), ((), ())),
                        preferred_element_type=jnp.float32,
                    )
                else:
                    summed = summed + jnp.dot(
                        window, kernel[tap_index], preferred_element_type=jnp.float32
                    )
    return summed.reshape(slot_count, 512, channels)


def tap_grads(tile_set, upstream):
    slot_count, channels = (tile_set.shape[0], tile_set.shape[-1])
    flat_rows = upstream.reshape(slot_count * 512, channels)
    result = []
    for step_x in range(3):
        for step_y in range(3):
            for step_z in range(3):
                window = tile_set[
                    :, step_x : step_x + 8, step_y : step_y + 8, step_z : step_z + 8, :
                ]
                window = window.reshape(slot_count * 512, channels)
                result.append(
                    lax.dot_general(
                        window,
                        flat_rows,
                        (((0,), (0,)), ((), ())),
                        preferred_element_type=jnp.float32,
                    )
                )
    return jnp.stack(result)


def widen_grid(dense_grid):
    widened = with_halo(dense_grid, (("gx", 0), ("gy", 1)), 1)
    return jnp.pad(widened, ((0, 0), (0, 0), (1, 1), (0, 0)))


def clip_factor(squares, channels):
    entries = 54.0 * channels * channels + channels
    return jnp.minimum(1.0, clip_level / jnp.sqrt(squares / entries + 1e-06))


def per_device(features, brick_pos, cotangent, first_kernel, second_kernel, norm_gain):
    slot_count, channels = (features.shape[0], features.shape[2])
    is_live = brick_pos < POS
    brick_x, brick_y, brick_z = brick_coords(jnp.minimum(brick_pos, POS - 1))
    put_x = jnp.where(is_live, brick_x, BX)
    live_mask = is_live[:, None, None]
    given_rows = jnp.where(live_mask, features, jnp.zeros_like(features))
    upstream = jnp.where(live_mask, cotangent, jnp.zeros_like(cotangent))

    def tiles_for(values):
        bricks = jnp.zeros((BX, BY, BZ, 8, 8, 8, channels), values.dtype)
        bricks = bricks.at[put_x, brick_y, brick_z].set(
            values.reshape(slot_count, 8, 8, 8, channels), mode="drop"
        )
        dense_grid = bricks.transpose(0, 3, 1, 4, 2, 5, 6).reshape(BX * 8, BY * 8, BZ * 8, channels)
        padded = widen_grid(dense_grid)

        def take_tile(start_x, start_y, start_z):
            return lax.dynamic_slice(
                padded, (start_x * 8, start_y * 8, start_z * 8, start_x * 0), (10, 10, 10, channels)
            )

        return jax.vmap(take_tile)(brick_x, brick_y, brick_z)

    given_tiles = tiles_for(given_rows)
    first_pre = jnp.where(live_mask, apply_taps(given_tiles, first_kernel, False), 0.0)
    hidden_full, pullback = jax.vjp(activate, first_pre, norm_gain)
    hidden = jnp.where(live_mask, hidden_full, 0.0).astype(jnp.bfloat16)
    hidden_tiles = tiles_for(hidden)
    second_pre = jnp.where(live_mask, apply_taps(hidden_tiles, second_kernel, False), 0.0)
    block_out = (given_rows.astype(jnp.float32) + second_pre).astype(jnp.bfloat16)
    second_grad = tap_grads(hidden_tiles, upstream).reshape(-1)
    hidden_grad = jnp.where(live_mask, apply_taps(tiles_for(upstream), second_kernel, True), 0.0)
    pre_full, gain_grad = pullback(hidden_grad)
    pre_grad = jnp.where(live_mask, pre_full, 0.0).astype(jnp.bfloat16)
    first_grad = tap_grads(given_tiles, pre_grad).reshape(-1)
    back_conv = apply_taps(tiles_for(pre_grad), first_kernel, True)
    feature_grad = jnp.where(live_mask, upstream.astype(jnp.float32) + back_conv, 0.0).astype(
        jnp.bfloat16
    )
    combined, gain_summed = lax.psum(
        (jnp.concatenate([first_grad, second_grad]), gain_grad), ("gx", "gy")
    )
    shrink = clip_factor(
        jnp.sum(combined * combined) + jnp.sum(gain_summed * gain_summed), channels
    )
    updated = shrink * combined
    kernel_update = updated.reshape(2, 27, channels, channels)
    return (block_out, feature_grad, kernel_update, shrink * gain_summed)


def solution(mesh):
    in_specs = (
        P(("gx", "gy"), None, None),
        P(("gx", "gy")),
        P(("gx", "gy"), None, None),
        P(),
        P(),
        P(),
    )
    out_specs = (P(("gx", "gy"), None, None), P(("gx", "gy"), None, None), P(), P())
    return jax.shard_map(
        per_device, mesh=mesh, in_specs=in_specs, out_specs=out_specs, check_vma=False
    )
```

profile of v0, /device:TPU:1, one launch (start us, length us, event | category | flops | bytes accessed | tf_op | source)
XLA Modules:
  0.0 379.1 jit_solution(3082905530294748665)
XLA Ops:
  11.2 4.0 %collective-permute-start.8 = (bf16[1,16,8,128]{3,2,1,0:T(8,128)(2,1)S(1)}, bf16[1,16,8,128]{3,2,1,0:T(8,128)(2,1)S(1)}, u32[]{:S(2)}, u32[]{:S(2)}) collective-permute-start(bf16[1,16,8,128]{3,2,1,0:T(8,128)(2,1)S(1)} %get-tuple-element.24), channel_id=1, source_target_pairs={{0,16},{16,32},{32,48},{48,64},{64,80},{80,96},{96,112},{1,17},{17... | collective-permute-start | bytes 98312 | tf_op jit(solution)/shard_map/ppermute | solution.py:23
  17.4 4.0 %collective-permute-start = (bf16[1,16,8,128]{3,2,1,0:T(8,128)(2,1)S(1)}, bf16[1,16,8,128]{3,2,1,0:T(8,128)(2,1)S(1)}, u32[]{:S(2)}, u32[]{:S(2)}) collective-permute-start(bf16[1,16,8,128]{3,2,1,0:T(8,128)(2,1)S(1)} %get-tuple-element.28), channel_id=1, source_target_pairs={{0,16},{16,32},{32,48},{48,64},{64,80},{80,96},{96,112},{1,17},{17... | collective-permute-start | bytes 98312 | tf_op jit(solution)/shard_map/ppermute | solution.py:23
  22.9 6.1 %collective-permute-start.10 = (bf16[18,1,8,128]{3,2,1,0:T(8,128)(2,1)S(1)}, bf16[18,1,8,128]{3,2,1,0:T(8,128)(2,1)S(1)}, u32[]{:S(2)}, u32[]{:S(2)}) collective-permute-start(bf16[18,1,8,128]{3,2,1,0:T(8,128)(2,1)S(1)} %get-tuple-element.16), channel_id=1, source_target_pairs={{0,1},{1,2},{2,3},{3,4},{4,5},{5,6},{6,7},{7,8},{8,9},{9,10},{10,1... | collective-permute-start | bytes 110600 | tf_op jit(solution)/shard_map/ppermute | solution.py:23
  28.9 1.9 collective-permute-start.11
  30.9 5.1 %collective-permute-start.2 = (bf16[18,1,8,128]{3,2,1,0:T(8,128)(2,1)S(1)}, bf16[18,1,8,128]{3,2,1,0:T(8,128)(2,1)S(1)}, u32[]{:S(2)}, u32[]{:S(2)}) collective-permute-start(bf16[18,1,8,128]{3,2,1,0:T(8,128)(2,1)S(1)} %get-tuple-element.20), channel_id=1, source_target_pairs={{0,1},{1,2},{2,3},{3,4},{4,5},{5,6},{6,7},{7,8},{8,9},{9,10},{10,1... | collective-permute-start | bytes 110600 | tf_op jit(solution)/shard_map/ppermute | solution.py:23
  36.0 1.9 collective-permute-start.3
  38.8 2.7 pad_slice_fusion.18
  61.0 2.5 multiply_reduce_fusion.1
  63.7 2.7 fusion.293
  78.2 2.3 fusion.62
  81.4 4.3 %collective-permute-start.4 = (bf16[1,16,8,128]{3,2,1,0:T(8,128)(2,1)S(1)}, bf16[1,16,8,128]{3,2,1,0:T(8,128)(2,1)S(1)}, u32[]{:S(2)}, u32[]{:S(2)}) collective-permute-start(bf16[1,16,8,128]{3,2,1,0:T(8,128)(2,1)S(1)} %get-tuple-element.26), channel_id=1, source_target_pairs={{0,16},{16,32},{32,48},{48,64},{64,80},{80,96},{96,112},{1,17},{17... | collective-permute-start | bytes 98312 | tf_op jit(solution)/shard_map/ppermute | solution.py:23
  87.0 73.8 %psum.15 = f32[128]{0:T(128)S(1)} all-reduce(f32[128]{0:T(128)S(1)} %copy-done.163), channel_id=1, replica_groups=mesh['gx'=8,'gy'=16] {'gx','gy'}, use_global_device_ids=true, to_apply=%region_11.12 | all-reduce | flops 128 | bytes 1024 | tf_op jit(solution)/shard_map/psum | solution.py:148
  166.8 4.4 %collective-permute-start.6 = (bf16[18,1,8,128]{3,2,1,0:T(8,128)(2,1)S(1)}, bf16[18,1,8,128]{3,2,1,0:T(8,128)(2,1)S(1)}, u32[]{:S(2)}, u32[]{:S(2)}) collective-permute-start(bf16[18,1,8,128]{3,2,1,0:T(8,128)(2,1)S(1)} %get-tuple-element.18), channel_id=1, source_target_pairs={{0,1},{1,2},{2,3},{3,4},{4,5},{5,6},{6,7},{7,8},{8,9},{9,10},{10,1... | collective-permute-start | bytes 110600 | tf_op jit(solution)/shard_map/ppermute | solution.py:23
  171.2 1.9 collective-permute-start.7
  173.8 5.1 %collective-permute-start.14 = (bf16[18,1,8,128]{3,2,1,0:T(8,128)(2,1)}, bf16[18,1,8,128]{3,2,1,0:T(8,128)(2,1)}, u32[]{:S(2)}, u32[]{:S(2)}) collective-permute-start(bf16[18,1,8,128]{3,2,1,0:T(8,128)(2,1)} %get-tuple-element.14), channel_id=1, source_target_pairs={{0,1},{1,2},{2,3},{3,4},{4,5},{5,6},{6,7},{7,8},{8,9},{9,10},{10,1... | collective-permute-start | bytes 110600 | tf_op jit(solution)/shard_map/ppermute | solution.py:23
  179.0 2.1 collective-permute-start.15
  182.1 1.8 gather_fusion.1
  184.0 2.7 pad_slice_fusion.36
  189.8 1.8 gather_fusion.3
  191.6 2.7 pad_slice_fusion
  204.7 2.0 pad_maximum_fusion
  226.3 136.5 %all-reduce.6.cloned.1.call-done = f32[884736]{0:T(1024)} async-done(((f32[884736]{0:T(1024)}), f32[884736]{0:T(1024)}) %all-reduce.6.cloned.1.call-update) | async-done | bytes 3538960 | tf_op jit(solution)/shard_map/psum | solution.py:148
  362.9 3.5 multiply_reduce_fusion
  368.3 4.0 %broadcast_multiply_fusion = f32[884736]{0:T(1024)} fusion(f32[884736]{0:T(1024)} %all-reduce.6.cloned.1.call-done, f32[]{:T(128)S(6)} %min.7), kind=kLoop, calls=%fused_computation.82 | loop fusion | flops 884736 | bytes 7077892 | tf_op jit(solution)/shard_map/mul | solution.py:154
  (563 shorter events, 80.3 us)
Async XLA Ops:
  7.2 355.7 %all-reduce.6.cloned.1.call-start = ((), (), s32[]{:S(2)}) async-start(), calls=%async_computation | async-start | bytes 7077888 | tf_op jit(solution)/shard_map/psum | solution.py:148
  7.9 35.2 %copy-start.155 = (s32[2]{0:T(128)}, s32[2]{0:T(128)S(1)}, u32[]{:S(2)}) copy-start(s32[2]{0:T(128)S(1)} %get-tuple-element.9) | copy-start | bytes 28
  8.6 14.2 %copy-start.156 = (pred[2]{0:T(512)(128)(4,1)}, pred[2]{0:T(512)(128)(4,1)S(1)}, u32[]{:S(2)}) copy-start(pred[2]{0:T(512)(128)(4,1)S(1)} %broadcast_compare_fusion) | copy-start | bytes 10
  11.2 11.6 %collective-permute-start.8 = (bf16[1,16,8,128]{3,2,1,0:T(8,128)(2,1)S(1)}, bf16[1,16,8,128]{3,2,1,0:T(8,128)(2,1)S(1)}, u32[]{:S(2)}, u32[]{:S(2)}) collective-permute-start(bf16[1,16,8,128]{3,2,1,0:T(8,128)(2,1)S(1)} %get-tuple-element.24), channel_id=1, source_target_pairs={{0,16},{16,32},{32,48},{48,64},{64,80},{80,96},{96,112},{1,17},{17... | collective-permute-start | bytes 98312 | tf_op jit(solution)/shard_map/ppermute | solution.py:23
  15.3 7.6 %collective-permute-start.9 = (bf16[1,16,8,128]{3,2,1,0:T(8,128)(2,1)S(1)}, bf16[1,16,8,128]{3,2,1,0:T(8,128)(2,1)S(1)}, u32[]{:S(2)}, u32[]{:S(2)}) collective-permute-start(bf16[1,16,8,128]{3,2,1,0:T(8,128)(2,1)S(1)} %get-tuple-element.25), channel_id=1, source_target_pairs={{16,0},{32,16},{48,32},{64,48},{80,64},{96,80},{112,96},{17,1},{33... | collective-permute-start | bytes 98312 | tf_op jit(solution)/shard_map/ppermute | solution.py:25
  17.4 13.4 %collective-permute-start = (bf16[1,16,8,128]{3,2,1,0:T(8,128)(2,1)S(1)}, bf16[1,16,8,128]{3,2,1,0:T(8,128)(2,1)S(1)}, u32[]{:S(2)}, u32[]{:S(2)}) collective-permute-start(bf16[1,16,8,128]{3,2,1,0:T(8,128)(2,1)S(1)} %get-tuple-element.28), channel_id=1, source_target_pairs={{0,16},{16,32},{32,48},{48,64},{64,80},{80,96},{96,112},{1,17},{17... | collective-permute-start | bytes 98312 | tf_op jit(solution)/shard_map/ppermute | solution.py:23
  21.4 9.4 %collective-permute-start.1 = (bf16[1,16,8,128]{3,2,1,0:T(8,128)(2,1)S(1)}, bf16[1,16,8,128]{3,2,1,0:T(8,128)(2,1)S(1)}, u32[]{:S(2)}, u32[]{:S(2)}) collective-permute-start(bf16[1,16,8,128]{3,2,1,0:T(8,128)(2,1)S(1)} %get-tuple-element.29), channel_id=1, source_target_pairs={{16,0},{32,16},{48,32},{64,48},{80,64},{96,80},{112,96},{17,1},{33... | collective-permute-start | bytes 98312 | tf_op jit(solution)/shard_map/ppermute | solution.py:25
  22.9 15.1 %collective-permute-start.10 = (bf16[18,1,8,128]{3,2,1,0:T(8,128)(2,1)S(1)}, bf16[18,1,8,128]{3,2,1,0:T(8,128)(2,1)S(1)}, u32[]{:S(2)}, u32[]{:S(2)}) collective-permute-start(bf16[18,1,8,128]{3,2,1,0:T(8,128)(2,1)S(1)} %get-tuple-element.16), channel_id=1, source_target_pairs={{0,1},{1,2},{2,3},{3,4},{4,5},{5,6},{6,7},{7,8},{8,9},{9,10},{10,1... | collective-permute-start | bytes 110600 | tf_op jit(solution)/shard_map/ppermute | solution.py:23
  28.9 9.1 %collective-permute-start.11 = (bf16[18,1,8,128]{3,2,1,0:T(8,128)(2,1)S(1)}, bf16[18,1,8,128]{3,2,1,0:T(8,128)(2,1)S(1)}, u32[]{:S(2)}, u32[]{:S(2)}) collective-permute-start(bf16[18,1,8,128]{3,2,1,0:T(8,128)(2,1)S(1)} %get-tuple-element.17), channel_id=1, source_target_pairs={{1,0},{2,1},{3,2},{4,3},{5,4},{6,5},{7,6},{8,7},{9,8},{10,9},{11,1... | collective-permute-start | bytes 110600 | tf_op jit(solution)/shard_map/ppermute | solution.py:25
  30.9 12.0 %collective-permute-start.2 = (bf16[18,1,8,128]{3,2,1,0:T(8,128)(2,1)S(1)}, bf16[18,1,8,128]{3,2,1,0:T(8,128)(2,1)S(1)}, u32[]{:S(2)}, u32[]{:S(2)}) collective-permute-start(bf16[18,1,8,128]{3,2,1,0:T(8,128)(2,1)S(1)} %get-tuple-element.20), channel_id=1, source_target_pairs={{0,1},{1,2},{2,3},{3,4},{4,5},{5,6},{6,7},{7,8},{8,9},{9,10},{10,1... | collective-permute-start | bytes 110600 | tf_op jit(solution)/shard_map/ppermute | solution.py:23
  36.0 6.8 %collective-permute-start.3 = (bf16[18,1,8,128]{3,2,1,0:T(8,128)(2,1)S(1)}, bf16[18,1,8,128]{3,2,1,0:T(8,128)(2,1)S(1)}, u32[]{:S(2)}, u32[]{:S(2)}) collective-permute-start(bf16[18,1,8,128]{3,2,1,0:T(8,128)(2,1)S(1)} %get-tuple-element.21), channel_id=1, source_target_pairs={{1,0},{2,1},{3,2},{4,3},{5,4},{6,5},{7,6},{8,7},{9,8},{10,9},{11,1... | collective-permute-start | bytes 110600 | tf_op jit(solution)/shard_map/ppermute | solution.py:25
  45.3 5.9 %copy-start.3 = (bf16[2,8,8,8,128]{4,3,2,1,0:T(8,128)(2,1)}, bf16[2,8,8,8,128]{4,3,2,1,0:T(8,128)(2,1)S(1)}, u32[]{:S(2)}) copy-start(bf16[2,8,8,8,128]{4,3,2,1,0:T(8,128)(2,1)S(1)} %get-tuple-element.127) | copy-start | bytes 786436
  78.2 8.8 %copy-start.163 = (f32[128]{0:T(128)S(1)}, f32[128]{0:T(128)}, u32[]{:S(2)}) copy-start(f32[128]{0:T(128)} %get-tuple-element.4) | copy-start | bytes 1540
  80.5 80.4 %copy-start.100 = (bf16[2,8,8,8,128]{4,3,2,1,0:T(8,128)(2,1)S(1)}, bf16[2,8,8,8,128]{4,3,2,1,0:T(8,128)(2,1)}, u32[]{:S(2)}) copy-start(bf16[2,8,8,8,128]{4,3,2,1,0:T(8,128)(2,1)} %get-tuple-element.12) | copy-start | bytes 786436
  81.4 85.4 %collective-permute-start.4 = (bf16[1,16,8,128]{3,2,1,0:T(8,128)(2,1)S(1)}, bf16[1,16,8,128]{3,2,1,0:T(8,128)(2,1)S(1)}, u32[]{:S(2)}, u32[]{:S(2)}) collective-permute-start(bf16[1,16,8,128]{3,2,1,0:T(8,128)(2,1)S(1)} %get-tuple-element.26), channel_id=1, source_target_pairs={{0,16},{16,32},{32,48},{48,64},{64,80},{80,96},{96,112},{1,17},{17... | collective-permute-start | bytes 98312 | tf_op jit(solution)/shard_map/ppermute | solution.py:23
  85.7 81.1 %collective-permute-start.5 = (bf16[1,16,8,128]{3,2,1,0:T(8,128)(2,1)S(1)}, bf16[1,16,8,128]{3,2,1,0:T(8,128)(2,1)S(1)}, u32[]{:S(2)}, u32[]{:S(2)}) collective-permute-start(bf16[1,16,8,128]{3,2,1,0:T(8,128)(2,1)S(1)} %get-tuple-element.27), channel_id=1, source_target_pairs={{16,0},{32,16},{48,32},{64,48},{80,64},{96,80},{112,96},{17,1},{33... | collective-permute-start | bytes 98312 | tf_op jit(solution)/shard_map/ppermute | solution.py:25
  160.8 6.0 %copy-start.161 = (f32[128]{0:T(128)}, f32[128]{0:T(128)S(1)}, u32[]{:S(2)}) copy-start(f32[128]{0:T(128)S(1)} %psum.15) | copy-start | bytes 1540
  164.2 9.0 %collective-permute-start.12 = (bf16[1,16,8,128]{3,2,1,0:T(8,128)(2,1)S(1)}, bf16[1,16,8,128]{3,2,1,0:T(8,128)(2,1)S(1)}, u32[]{:S(2)}, u32[]{:S(2)}) collective-permute-start(bf16[1,16,8,128]{3,2,1,0:T(8,128)(2,1)S(1)} %get-tuple-element.22), channel_id=1, source_target_pairs={{0,16},{16,32},{32,48},{48,64},{64,80},{80,96},{96,112},{1,17},{17... | collective-permute-start | bytes 98312 | tf_op jit(solution)/shard_map/ppermute | solution.py:23
  165.4 7.7 %collective-permute-start.13 = (bf16[1,16,8,128]{3,2,1,0:T(8,128)(2,1)S(1)}, bf16[1,16,8,128]{3,2,1,0:T(8,128)(2,1)S(1)}, u32[]{:S(2)}, u32[]{:S(2)}) collective-permute-start(bf16[1,16,8,128]{3,2,1,0:T(8,128)(2,1)S(1)} %get-tuple-element.23), channel_id=1, source_target_pairs={{16,0},{32,16},{48,32},{64,48},{80,64},{96,80},{112,96},{17,1},{33... | collective-permute-start | bytes 98312 | tf_op jit(solution)/shard_map/ppermute | solution.py:25
  166.8 14.3 %collective-permute-start.6 = (bf16[18,1,8,128]{3,2,1,0:T(8,128)(2,1)S(1)}, bf16[18,1,8,128]{3,2,1,0:T(8,128)(2,1)S(1)}, u32[]{:S(2)}, u32[]{:S(2)}) collective-permute-start(bf16[18,1,8,128]{3,2,1,0:T(8,128)(2,1)S(1)} %get-tuple-element.18), channel_id=1, source_target_pairs={{0,1},{1,2},{2,3},{3,4},{4,5},{5,6},{6,7},{7,8},{8,9},{9,10},{10,1... | collective-permute-start | bytes 110600 | tf_op jit(solution)/shard_map/ppermute | solution.py:23
  171.2 9.9 %collective-permute-start.7 = (bf16[18,1,8,128]{3,2,1,0:T(8,128)(2,1)S(1)}, bf16[18,1,8,128]{3,2,1,0:T(8,128)(2,1)S(1)}, u32[]{:S(2)}, u32[]{:S(2)}) collective-permute-start(bf16[18,1,8,128]{3,2,1,0:T(8,128)(2,1)S(1)} %get-tuple-element.19), channel_id=1, source_target_pairs={{1,0},{2,1},{3,2},{4,3},{5,4},{6,5},{7,6},{8,7},{9,8},{10,9},{11,1... | collective-permute-start | bytes 110600 | tf_op jit(solution)/shard_map/ppermute | solution.py:25
  173.8 14.2 %collective-permute-start.14 = (bf16[18,1,8,128]{3,2,1,0:T(8,128)(2,1)}, bf16[18,1,8,128]{3,2,1,0:T(8,128)(2,1)}, u32[]{:S(2)}, u32[]{:S(2)}) collective-permute-start(bf16[18,1,8,128]{3,2,1,0:T(8,128)(2,1)} %get-tuple-element.14), channel_id=1, source_target_pairs={{0,1},{1,2},{2,3},{3,4},{4,5},{5,6},{6,7},{7,8},{8,9},{9,10},{10,1... | collective-permute-start | bytes 110600 | tf_op jit(solution)/shard_map/ppermute | solution.py:23
  179.0 9.0 %collective-permute-start.15 = (bf16[18,1,8,128]{3,2,1,0:T(8,128)(2,1)}, bf16[18,1,8,128]{3,2,1,0:T(8,128)(2,1)}, u32[]{:S(2)}, u32[]{:S(2)}) collective-permute-start(bf16[18,1,8,128]{3,2,1,0:T(8,128)(2,1)} %get-tuple-element.15), channel_id=1, source_target_pairs={{1,0},{2,1},{3,2},{4,3},{5,4},{6,5},{7,6},{8,7},{9,8},{10,9},{11,1... | collective-permute-start | bytes 110600 | tf_op jit(solution)/shard_map/ppermute | solution.py:25
  226.3 141.4 %copy-start.162 = (f32[128]{0:T(128)S(1)}, f32[128]{0:T(128)}, u32[]{:S(2)}) copy-start(f32[128]{0:T(128)} %copy-done.161) | copy-start | bytes 1540
  (157 other events, 272.5 us)
Sparse Core Ops, SparseCore 0:
  206.9 155.9 all-reduce.5
where the time goes:
time: 381 us; the launch traced here: 379 us
  waiting for transfers between devices  137 us (36%)
  blocking collectives  73.8 us (19%)
  starting transfers between devices  47.4 us (12%)
  matrix products  43.2 us (11%)
  local copies, waits for them, and re-layouts  33.8 us (9%)
  other arithmetic  25.6 us (7%)
  between operations  18.7 us (5%)
    psum x1, waiting for transfers between devices, per_device(): lax.psum((jnp.concatenate([first_grad, second_grad]), gain_grad), ('gx',...  137 us
    psum x1, blocking collectives, per_device(): lax.psum((jnp.concatenate([first_grad, second_grad]), gain_grad), ('gx',...  73.8 us
    ppermute x8, starting transfers between devices, with_halo(): lax.ppermute(tail, axis, [(i, (i + 1) % count) for i in range(ends)])  34.3 us
    dot_general x54, matrix products, tap_grads(): lax.dot_general(window, flat_rows, (((0,), (0,)), ((), ())), preferred_el...  15.4 us
    dot_general x54, matrix products, apply_taps(): lax.dot_general(window, kernel[tap_index], (((1,), (1,)), ((), ())), pref...  14.3 us
    slice x8, local copies, waits for them, and re-layouts, apply_taps(): tile_set[:, start_x:start_x + 8, start_y:start_y + 8, start_z:start_z + 8...  13.6 us
    dot_general x54, matrix products, apply_taps(): jnp.dot(window, kernel[tap_index], preferred_element_type=jnp.float32)  13.4 us
    ppermute x8, starting transfers between devices, with_halo(): lax.ppermute(head, axis, [((i + 1) % count, i) for i in range(ends)])  13.1 us
  transfers between devices with their start and end apart: 17, of which 1 were waited for; matrix products, arithmetic and copies ran while one was open for 8% of the time, Pallas kernels for 0%

commit v1 on v0

v1 whole, which is shorter than its diff:
```python
import jax
import jax.numpy as jnp
from jax import lax
from jax.experimental import pallas as pl
from jax.experimental.pallas import tpu as pltpu
from jax.sharding import PartitionSpec as P

MESH = pl.DeviceIdType.MESH
F32 = jnp.float32
BF16 = jnp.bfloat16
CLIP = 0.5
C = 128
POS = 4
DIRS = [(dx, dy) for dx in (-1, 0, 1) for dy in (-1, 0, 1) if (dx, dy) != (0, 0)]
ORDERS = [(0, 1, 2), (1, 2, 0), (2, 0, 1)]
NT = (((1,), (1,)), ((), ()))


def span(d, size, halo):
    if d == 0:
        return pl.ds(1, 16)
    if d < 0:
        return pl.ds(0 if halo else 1, 1)
    return pl.ds(17 if halo else 16, 1)


def step_kernel(
    pos_ref, gain_ref, feat_hbm, cot_hbm, k1_hbm, k2_hbm,
    out_hbm, fgrad_hbm, full_ref, stats_ref,
    feat, cot, w1, w2, r1, r2, grid1, grid2, ag, au, ah, ap,
    hid, pgr, outv, part, rcore, sa, ra, sb, rb, rc, gains,
    in_sem, out_sem, hs, hr, cs, cr, as_, ar, bs, br, zs, zr, ebs, ebr, eas, ear, ecs, ecr, gs, gr,
):
    gx = lax.axis_index("gx")
    gy = lax.axis_index("gy")
    core = gy % 2
    coord = ((gy // 2) % 2 * 2 + gx // 4, gx % 4, gy // 4)

    def peer(axis, value):
        x, y, z = (value if i == axis else coord[i] for i in range(3))
        return (x % 2 * 4 + y, z * 4 + x // 2 * 2 + core)

    sibling = (gx, gy + 1 - 2 * core)

    def there(d):
        x, y = gx + d[0], gy + d[1]
        return (x >= 0) & (x < 8) & (y >= 0) & (y < 16)

    def load(i, src, dst):
        return pltpu.make_async_copy(src, dst, in_sem.at[i])

    loads = [load(0, feat_hbm, feat), load(1, cot_hbm, cot), load(2, k1_hbm, w1), load(3, k2_hbm, w2)]
    for c in loads:
        c.start()

    for g in (grid1, grid2):
        for f in range(2):
            for e in (0, 17):
                g[f, e] = jnp.zeros((18, 8, C), BF16)
                for x in range(1, 17):
                    g[f, x, e] = jnp.zeros((8, C), BF16)

    barrier = pltpu.get_barrier_semaphore()
    for d in DIRS:
        @pl.when(there(d))
        def _():
            pl.semaphore_signal(barrier, inc=1, device_id=(gx + d[0], gy + d[1]), device_id_type=MESH)
    for axis in range(3):
        for k in (1, 2, 3):
            pl.semaphore_signal(barrier, inc=1, device_id=peer(axis, (coord[axis] + k) % 4), device_id_type=MESH)
    pl.semaphore_signal(barrier, inc=1, device_id=sibling, device_id_type=MESH)

    p0, p1 = pos_ref[0], pos_ref[1]
    where = [jnp.minimum(p0, POS - 1), jnp.minimum(p1, POS - 1)]
    bx = [w // 2 for w in where]
    by = [w % 2 for w in where]
    live = [(p0 < POS).astype(F32), (p1 < POS).astype(F32)]

    def place(grid, f, source):
        for p in range(POS):
            m0, m1 = (p0 == p).astype(F32), (p1 == p).astype(F32)
            for x in range(8):
                rows = pl.ds(x * 64, 64)
                v = source[0, rows].astype(F32) * m0 + source[1, rows].astype(F32) * m1
                grid[f, 1 + p // 2 * 8 + x, pl.ds(1 + p % 2 * 8, 8)] = v.reshape(8, 8, C).astype(BF16)

    def halo(phase, grid):
        def copies(d):
            i = DIRS.index(d)
            return pltpu.make_async_remote_copy(
                src_ref=grid.at[:, span(d[0], 16, False), span(d[1], 16, False)],
                dst_ref=grid.at[:, span(-d[0], 16, True), span(-d[1], 16, True)],
                send_sem=hs.at[phase, i], recv_sem=hr.at[phase, i],
                device_id=(gx + d[0], gy + d[1]), device_id_type=MESH,
            )

        def start():
            for d in DIRS:
                @pl.when(there(d))
                def _():
                    copies(d).start()

        def arrive():
            for d in DIRS:
                @pl.when(there((-d[0], -d[1])))
                def _():
                    copies(d).wait_recv()

        def done():
            for d in DIRS:
                @pl.when(there(d))
                def _():
                    copies(d).wait_send()

        return start, arrive, done

    start1, arrive1, done1 = halo(0, grid1)
    start2, arrive2, done2 = halo(1, grid2)

    loads[0].wait()
    loads[1].wait()
    place(grid1, 0, feat)
    place(grid1, 1, cot)

    expected = 10
    for d in DIRS:
        expected = expected + there(d).astype(jnp.int32)
    pl.semaphore_wait(barrier, expected)
    start1()

    loads[2].wait()
    loads[3].wait()
    for w, r in ((w2, r2), (w1, r1)):
        for t in range(27):
            r[t // 9, :, pl.ds(t % 9 * C, C)] = w[26 - t]

    z = lax.broadcasted_iota(jnp.int32, (10, 8, C), 1)
    first, last = z == 0, z == 7

    def gather(a, s, grid, f):
        def layer(x, carry):
            t = grid[f, bx[s] * 8 + x, pl.ds(by[s] * 8, 10)].astype(F32)
            down = jnp.where(first, 0.0, pltpu.roll(t, 1, 1))
            up = jnp.where(last, 0.0, pltpu.roll(t, 7, 1))
            for oz, v in enumerate((down, t, up)):
                for oy in range(3):
                    a[s, pl.ds(pl.multiple_of(x * 64, 64), 64), pl.ds((oy * 3 + oz) * C, C)] = (
                        v[oy : oy + 8].reshape(64, C).astype(BF16)
                    )
            return carry

        lax.fori_loop(0, 10, layer, 0)

    def conv(a, s, w):
        total = None
        for ox in range(3):
            v = jnp.dot(a[s, pl.ds(ox * 64, 512)], w[pl.ds(ox * 9, 9)].reshape(9 * C, C), preferred_element_type=F32)
            total = v if total is None else total + v
        return total

    def conv_t(a, s, r):
        total = None
        for ox in range(3):
            v = lax.dot_general(a[s, pl.ds(ox * 64, 512)], r[ox], NT, preferred_element_type=F32)
            total = v if total is None else total + v
        return total

    arrive1()
    gain = gain_ref[0:1, :]
    ggrad = jnp.zeros((1, C), F32)
    hid_t, pgr_t = [], []
    for s in range(2):
        gather(ag, s, grid1, 0)
        gather(au, s, grid1, 1)
        pre = conv(ag, s, w1)
        hgrad = conv_t(au, s, r2) * live[s]
        center = pre - jnp.mean(pre, axis=-1, keepdims=True)
        inv = lax.rsqrt(jnp.mean(center * center, axis=-1, keepdims=True) + 1e-05)
        unit = center * inv
        normed = unit * gain
        sig = jax.nn.sigmoid(normed)
        hidden = normed * sig * live[s]
        dn = hgrad * (sig * (1.0 + normed * (1.0 - sig)))
        ggrad = ggrad + jnp.sum(dn * unit, axis=0, keepdims=True)
        du = dn * gain
        dc = inv * (du - unit * jnp.mean(du * unit, axis=-1, keepdims=True))
        pg = (dc - jnp.mean(dc, axis=-1, keepdims=True)) * live[s]
        hid[s] = hidden.astype(BF16)
        pgr[s] = pg.astype(BF16)
        hid_t.append(hidden.T.astype(BF16))
        pgr_t.append(pg.T.astype(BF16))

    place(grid2, 0, hid)
    place(grid2, 1, pgr)
    start2()

    def gain_copy(stage, k):
        if stage == 0:
            return pltpu.make_async_remote_copy(
                src_ref=gains.at[0, 0], dst_ref=gains.at[0, 1], send_sem=gs.at[0], recv_sem=gr.at[0],
                device_id=sibling, device_id_type=MESH)
        axis = stage - 1
        i = 1 + axis * 3 + k - 1
        return pltpu.make_async_remote_copy(
            src_ref=gains.at[stage, coord[axis]], dst_ref=gains.at[stage, coord[axis]],
            send_sem=gs.at[i], recv_sem=gr.at[i],
            device_id=peer(axis, (coord[axis] + k) % 4), device_id_type=MESH)

    gains[0, 0] = jnp.broadcast_to(ggrad, (8, C))
    gain_copy(0, 0).start()

    half = pl.multiple_of(core * 64, 64)
    other = pl.multiple_of((1 - core) * 64, 64)

    def core_copy(g):
        return pltpu.make_async_remote_copy(
            src_ref=part.at[pl.ds(g * 9, 9), pl.ds(other, 64)], dst_ref=rcore.at[pl.ds(g * 9, 9)],
            send_sem=cs.at[g], recv_sem=cr.at[g], device_id=sibling, device_id_type=MESH)

    def group(g):
        if g < 3:
            a, lhs, ox = au, hid_t, 2 - g
        else:
            a, lhs, ox = ag, pgr_t, g - 3
        v = (jnp.dot(lhs[0], a[0, pl.ds(ox * 64, 512)], preferred_element_type=F32)
             + jnp.dot(lhs[1], a[1, pl.ds(ox * 64, 512)], preferred_element_type=F32))
        for k in range(9):
            if g < 3:
                part[g * 9 + 8 - k] = v[:, k * C : (k + 1) * C]
            else:
                part[g * 9 + k] = v[:, k * C : (k + 1) * C].T
        core_copy(g).start()

    def axes(i):
        return ORDERS[i]

    def piece(i):
        a, b, _ = axes(i)
        return coord[a], coord[b] // 2, coord[b] % 2

    def send_a(i, k):
        a = axes(i)[0]
        to = (coord[a] + k) % 4
        return pltpu.make_async_remote_copy(
            src_ref=sa.at[pl.ds(i * 18, 18), to], dst_ref=ra.at[i, k - 1],
            send_sem=as_.at[i * 3 + k - 1], recv_sem=ar.at[i * 3 + k - 1],
            device_id=peer(a, to), device_id_type=MESH)

    def send_b(i, k):
        b = axes(i)[1]
        to = (coord[b] + k) % 4
        return pltpu.make_async_remote_copy(
            src_ref=sb.at[i, pl.ds(to // 2 * 9, 9), to % 2], dst_ref=rb.at[i, k - 1],
            send_sem=bs.at[i * 3 + k - 1], recv_sem=br.at[i * 3 + k - 1],
            device_id=peer(b, to), device_id_type=MESH)

    def send_c(i, k):
        c = axes(i)[2]
        to = (coord[c] + k) % 4
        return pltpu.make_async_remote_copy(
            src_ref=rc.at[i, coord[c]], dst_ref=rc.at[i, coord[c]],
            send_sem=zs.at[i * 3 + k - 1], recv_sem=zr.at[i * 3 + k - 1],
            device_id=peer(c, to), device_id_type=MESH)

    def share_b(i, k):
        b = axes(i)[1]
        pa, hi, lo = piece(i)
        place_ = full_ref.at[pl.ds(i * 18 + hi * 9, 9), core * 8 + pa * 2 + lo]
        return pltpu.make_async_remote_copy(
            src_ref=place_, dst_ref=place_, send_sem=ebs.at[i * 3 + k - 1], recv_sem=ebr.at[i * 3 + k - 1],
            device_id=peer(b, (coord[b] + k) % 4), device_id_type=MESH)

    def share_a(i, k):
        a = axes(i)[0]
        place_ = full_ref.at[pl.ds(i * 18, 18), pl.ds(core * 8 + coord[a] * 2, 2)]
        return pltpu.make_async_remote_copy(
            src_ref=place_, dst_ref=place_, send_sem=eas.at[i * 3 + k - 1], recv_sem=ear.at[i * 3 + k - 1],
            device_id=peer(a, (coord[a] + k) % 4), device_id_type=MESH)

    def share_core(i):
        place_ = full_ref.at[pl.ds(i * 18, 18), pl.ds(core * 8, 8)]
        return pltpu.make_async_remote_copy(
            src_ref=place_, dst_ref=place_, send_sem=ecs.at[i], recv_sem=ecr.at[i],
            device_id=sibling, device_id_type=MESH)

    def reduce_core(i):
        for g in (2 * i, 2 * i + 1):
            core_copy(g).wait_recv()

        def tap(t, carry):
            v = part[t, pl.ds(half, 64)] + rcore[t]
            rcore[t] = v
            sa[t] = v.reshape(4, 16, C).astype(BF16)
            return carry

        lax.fori_loop(i * 18, i * 18 + 18, tap, 0)
        for k in (1, 2, 3):
            send_a(i, k).start()

    def reduce_a(i):
        for k in (1, 2, 3):
            send_a(i, k).wait_recv()
        mine = pl.multiple_of(coord[axes(i)[0]] * 16, 16)
        v = rcore[pl.ds(i * 18, 18), pl.ds(mine, 16)]
        for k in range(3):
            v = v + ra[i, k].astype(F32)
        sb[i] = v.reshape(18, 2, 8, C)
        for k in (1, 2, 3):
            send_b(i, k).start()

    def reduce_b(i):
        for k in (1, 2, 3):
            send_b(i, k).wait_recv()
        _, hi, lo = piece(i)
        v = sb[i, pl.ds(hi * 9, 9), lo]
        for k in range(3):
            v = v + rb[i, k]
        rc[i, coord[axes(i)[2]]] = v
        for k in (1, 2, 3):
            send_c(i, k).start()

    def reduce_c(i):
        for k in (1, 2, 3):
            send_c(i, k).wait_recv()
        pa, hi, lo = piece(i)
        v = ((rc[i, 0] + rc[i, 1]) + rc[i, 2]) + rc[i, 3]
        full_ref[pl.ds(i * 18 + hi * 9, 9), core * 8 + pa * 2 + lo] = v.astype(BF16)
        for k in (1, 2, 3):
            share_b(i, k).start()

    def spread_a(i):
        for k in (1, 2, 3):
            share_b(i, k).wait_recv()
        for k in (1, 2, 3):
            share_a(i, k).start()

    def spread_core(i):
        for k in (1, 2, 3):
            share_a(i, k).wait_recv()
        share_core(i).start()

    def gain_step(stage):
        if stage == 0:
            gain_copy(0, 0).wait_recv()
            gains[1, coord[0]] = gains[0, 0] + gains[0, 1]
        else:
            for k in (1, 2, 3):
                gain_copy(stage, k).wait_recv()
            v = ((gains[stage, 0] + gains[stage, 1]) + gains[stage, 2]) + gains[stage, 3]
            if stage == 3:
                return v
            gains[stage + 1, coord[stage]] = v
        for k in (1, 2, 3):
            gain_copy(stage + 1, k).start()

    def second_half(s, f):
        if f == 0:
            gather(ah, s, grid2, 0)
            v = conv(ah, s, w2) * live[s] + feat[s].astype(F32) * live[s]
        else:
            gather(ap, s, grid2, 1)
            v = (conv_t(ap, s, r1) + cot[s].astype(F32)) * live[s]
        outv[f, s] = v.astype(BF16)

    group(0)
    group(1)
    gain_step(0)
    group(2)
    group(3)
    reduce_core(0)
    group(4)
    group(5)
    reduce_core(1)
    gain_step(1)
    arrive2()
    reduce_core(2)
    second_half(0, 0)
    reduce_a(0)
    reduce_a(1)
    gain_step(2)
    second_half(1, 0)
    reduce_b(0)
    reduce_a(2)
    reduce_b(1)
    second_half(0, 1)
    reduce_c(0)
    reduce_b(2)
    reduce_c(1)
    second_half(1, 1)
    out_copies = [pltpu.make_async_copy(outv.at[0], out_hbm, out_sem.at[0]),
                  pltpu.make_async_copy(outv.at[1], fgrad_hbm, out_sem.at[1])]
    for c in out_copies:
        c.start()
    spread_a(0)
    reduce_c(2)
    spread_a(1)
    gain_sum = gain_step(3)
    spread_core(0)
    spread_a(2)
    spread_core(1)

    def squares(i, acc):
        share_core(i).wait_recv()

        def tap(t, acc):
            v = full_ref[t].astype(F32)
            return acc + jnp.sum(v * v, axis=0)

        return lax.fori_loop(i * 18, i * 18 + 18, tap, acc)

    acc = jnp.zeros((8, C), F32)
    acc = squares(0, acc)
    spread_core(2)
    acc = squares(1, acc)
    acc = squares(2, acc)
    total = jnp.sum(acc) + jnp.sum(gain_sum[0:1] * gain_sum[0:1])
    entries = 54.0 * C * C + C
    mean = jnp.full((8, C), total / entries + 1e-06, F32)
    shrink = jnp.minimum(1.0, CLIP / jnp.sqrt(mean))
    stats_ref[0] = shrink
    stats_ref[1] = shrink * gain_sum

    done1()
    done2()
    for c in out_copies:
        c.wait()
    for g in range(6):
        core_copy(g).wait_send()
    gain_copy(0, 0).wait_send()
    for k in (1, 2, 3):
        for stage in (1, 2, 3):
            gain_copy(stage, k).wait_send()
        for i in range(3):
            for send in (send_a, send_b, send_c, share_b, share_a):
                send(i, k).wait_send()
    for i in range(3):
        share_core(i).wait_send()


def finish_kernel(full_ref, stats_ref, out_ref):
    v = full_ref[...].astype(F32).reshape(9, 128, C)
    out_ref[...] = v * stats_ref[0, 0:1, :]


def per_device(features, brick_pos, cotangent, first_kernel, second_kernel, norm_gain):
    hbm = pl.BlockSpec(memory_space=pl.ANY)
    vmem = pl.BlockSpec(memory_space=pltpu.VMEM)
    dma = pltpu.SemaphoreType.DMA
    V = pltpu.VMEM
    tile = (2, 640, 9 * C)
    out, fgrad, full, stats = pl.pallas_call(
        step_kernel,
        out_shape=(
            jax.ShapeDtypeStruct((2, 512, C), BF16),
            jax.ShapeDtypeStruct((2, 512, C), BF16),
            jax.ShapeDtypeStruct((54, 16, 8, C), BF16),
            jax.ShapeDtypeStruct((2, 8, C), F32),
        ),
        in_specs=[pl.BlockSpec(memory_space=pltpu.SMEM), vmem, hbm, hbm, hbm, hbm],
        out_specs=(hbm, hbm, vmem, vmem),
        scratch_shapes=[
            V((2, 512, C), BF16), V((2, 512, C), BF16),
            V((27, C, C), BF16), V((27, C, C), BF16),
            V((3, C, 9 * C), BF16), V((3, C, 9 * C), BF16),
            V((2, 18, 18, 8, C), BF16), V((2, 18, 18, 8, C), BF16),
            V(tile, BF16), V(tile, BF16), V(tile, BF16), V(tile, BF16),
            V((2, 512, C), BF16), V((2, 512, C), BF16), V((2, 2, 512, C), BF16),
            V((54, C, C), F32), V((54, 64, C), F32),
            V((54, 4, 16, C), BF16), V((3, 3, 18, 16, C), BF16),
            V((3, 18, 2, 8, C), F32), V((3, 3, 9, 8, C), F32), V((3, 4, 9, 8, C), F32),
            V((4, 4, 8, C), F32),
            dma((4,)), dma((2,)), dma((2, 8)), dma((2, 8)), dma((6,)), dma((6,)),
            dma((9,)), dma((9,)), dma((9,)), dma((9,)), dma((9,)), dma((9,)),
            dma((9,)), dma((9,)), dma((9,)), dma((9,)), dma((3,)), dma((3,)), dma((10,)), dma((10,)),
        ],
        compiler_params=pltpu.CompilerParams(
            collective_id=0, has_side_effects=True, vmem_limit_bytes=56 * 2**20
        ),
        name="step",
    )(brick_pos, norm_gain.reshape(1, C), features, cotangent, first_kernel, second_kernel)
    update = pl.pallas_call(
        finish_kernel,
        grid=(6,),
        out_shape=jax.ShapeDtypeStruct((54, C, C), F32),
        in_specs=[
            pl.BlockSpec((9, 16, 8, C), lambda i: ((i + 3) % 6, 0, 0, 0)),
            pl.BlockSpec((2, 8, C), lambda i: (0, 0, 0)),
        ],
        out_specs=pl.BlockSpec((9, C, C), lambda i: (i, 0, 0)),
        compiler_params=pltpu.CompilerParams(vmem_limit_bytes=8 * 2**20),
        name="finish",
    )(full, stats)
    return out, fgrad, update.reshape(2, 27, C, C), stats[1, 0]


def solution(mesh):
    rows = P(("gx", "gy"), None, None)
    return jax.shard_map(
        per_device, mesh=mesh, in_specs=(rows, P(("gx", "gy")), rows, P(), P(), P()),
        out_specs=(rows, rows, P(), P()), check_vma=False,
    )
```

time: 381 us -> 64.1 us (0.17)
  waiting for transfers between devices: 137 us -> 0 us
  blocking collectives: 73.8 us -> 0 us
  Pallas kernels: 0 us -> 58.5 us
  starting transfers between devices: 47.4 us -> 0 us
  matrix products: 43.2 us -> 0 us
  local copies, waits for them, and re-layouts: 33.8 us -> 4.76 us
  other arithmetic: 25.6 us -> 0 us
  between operations: 18.7 us -> 0.65 us
    psum x1 -> x0, waiting for transfers between devices: 137 us -> none  [per_device(): lax.psum((jnp.concatenate([first_grad, second_grad]), gain_grad), ('gx',...]
    psum x1 -> x0, blocking collectives: 73.8 us -> none  [per_device(): lax.psum((jnp.concatenate([first_grad, second_grad]), gain_grad), ('gx',...]
    pallas_call x0 -> x2, Pallas kernels: none -> 58.5 us  [the longest x1 55.7 us: per_device(): pl.pallas_call(step_kernel, out_shape=(jax.ShapeDtypeStruct((2, 512, C),...]
    ppermute x16 -> x0, starting transfers between devices: 47.4 us -> none  [the longest x8 34.3 us: with_halo(): lax.ppermute(tail, axis, [(i, (i + 1) % count) for i in range(ends)])]
    dot_general x162 -> x0, matrix products: 43.2 us -> none  [the longest x54 15.4 us: tap_grads(): lax.dot_general(window, flat_rows, (((0,), (0,)), ((), ())), preferred_el...]
    slice x12 -> x0, local copies, waits for them, and re-layouts: 13.7 us -> none  [the longest x8 13.6 us: apply_taps(): tile_set[:, start_x:start_x + 8, start_y:start_y + 8, start_z:start_z + 8...]
    reduce_sum x4 -> x0, other arithmetic: 7.32 us -> none  [the longest x1 3.51 us: per_device(): jnp.sum(combined * combined) + jnp.sum(gain_summed * gain_summed)]
    unnamed x328 -> x10, local copies, waits for them, and re-layouts: 10.4 us -> 3.58 us
  transfers between devices with their start and end apart: 17 -> 0, of which waited for: 1 -> 0; matrix products, arithmetic and copies ran while one was open for 8% -> 0% of each run, Pallas kernels for 0% -> 0%
where the time goes in v1:
time: 64.1 us; the launch traced here: 63.9 us
  Pallas kernels  58.5 us (91%)
  local copies, waits for them, and re-layouts  4.76 us (7%)
  between operations  0.65 us (1%)
    pallas_call x1, Pallas kernels, per_device(): pl.pallas_call(step_kernel, out_shape=(jax.ShapeDtypeStruct((2, 512, C),...  55.7 us
    unnamed x10, local copies, waits for them, and re-layouts  3.58 us
    pallas_call x1, Pallas kernels, per_device(): pl.pallas_call(finish_kernel, grid=(6,), out_shape=jax.ShapeDtypeStruct((...  2.76 us

profile of v1, /device:TPU:1, one launch (start us, length us, event | category | flops | bytes accessed | tf_op | source)
XLA Modules:
  0.0 63.9 jit_solution(18267824071809441743)
XLA Ops:
  0.6 55.7 %step.1 = (bf16[2,512,128]{2,1,0:T(8,128)(2,1)}, bf16[2,512,128]{2,1,0:T(8,128)(2,1)}, bf16[54,16,8,128]{3,2,1,0:T(8,128)(2,1)}, f32[2,8,128]{2,1,0:T(8,128)}) custom-call(s32[2]{0:T(128)} %pos_ref.1, f32[1,128]{1,0:T(1,128)} %bitcast.5, bf16[2,512,128]{2,1,0:T(8,128)(2,1)} %feat_hbm.1, bf16[2,512,128]{2,1,0:T(8,128)(2,1)} %cot_hbm.1, ...), custom_call_target="tpu_custom_call" | custom-call | tf_op jit(solution)/shard_map/step/pallas_call | solution.py:451
  56.3 0.0 copy-start
  56.3 1.5 %copy-done = bf16[54,16,8,128]{3,2,1,0:T(8,128)(2,1)S(1)} copy-done((bf16[54,16,8,128]{3,2,1,0:T(8,128)(2,1)S(1)}, bf16[54,16,8,128]{3,2,1,0:T(8,128)(2,1)}, u32[]{:S(2)}) %copy-start) | copy-done | bytes 1769496
  57.8 0.0 copy-start.1
  57.8 0.7 %copy-done.1 = f32[2,8,128]{2,1,0:T(8,128)S(1)} copy-done((f32[2,8,128]{2,1,0:T(8,128)S(1)}, f32[2,8,128]{2,1,0:T(8,128)}, u32[]{:S(2)}) %copy-start.1) | copy-done | bytes 8216
  58.5 0.0 copy-start.3
  58.5 0.0 copy-start.2
  58.5 2.8 %finish.1 = f32[54,128,128]{2,1,0:T(8,128)} custom-call(bf16[54,16,8,128]{3,2,1,0:T(8,128)(2,1)S(1)} %copy-done, f32[2,8,128]{2,1,0:T(8,128)S(1)} %copy-done.1), custom_call_target="tpu_custom_call" | custom-call | tf_op jit(solution)/shard_map/finish/pallas_call | solution.py:481
  61.3 1.2 %slice_bitcast_fusion = f32[128]{0:T(128)} fusion(f32[2,8,128]{2,1,0:T(8,128)} %get-tuple-element.11.stats_ref), kind=kLoop, calls=%fused_computation | loop fusion | bytes 1024 | tf_op jit(solution)/shard_map/squeeze | solution.py:493
  62.5 0.0 copy-done.3
  62.5 0.7 %copy.12 = bf16[2,512,128]{2,1,0:T(8,128)(2,1)} copy(bf16[2,512,128]{2,1,0:T(8,128)(2,1)S(1)} %copy-done.3) | data formatting | bytes 524288
  63.2 0.0 copy-done.2
  63.2 0.7 %copy.13 = bf16[2,512,128]{2,1,0:T(8,128)(2,1)} copy(bf16[2,512,128]{2,1,0:T(8,128)(2,1)S(1)} %copy-done.2) | data formatting | bytes 524288
Async XLA Ops:
  56.3 1.5 %copy-start = (bf16[54,16,8,128]{3,2,1,0:T(8,128)(2,1)S(1)}, bf16[54,16,8,128]{3,2,1,0:T(8,128)(2,1)}, u32[]{:S(2)}) copy-start(bf16[54,16,8,128]{3,2,1,0:T(8,128)(2,1)} %get-tuple-element.10.full_ref) | copy-start | bytes 5308420
  57.8 0.7 %copy-start.1 = (f32[2,8,128]{2,1,0:T(8,128)S(1)}, f32[2,8,128]{2,1,0:T(8,128)}, u32[]{:S(2)}) copy-start(f32[2,8,128]{2,1,0:T(8,128)} %get-tuple-element.11.stats_ref) | copy-start | bytes 24580
  58.5 3.9 %copy-start.3 = (bf16[2,512,128]{2,1,0:T(8,128)(2,1)S(1)}, bf16[2,512,128]{2,1,0:T(8,128)(2,1)}, u32[]{:S(2)}) copy-start(bf16[2,512,128]{2,1,0:T(8,128)(2,1)} %get-tuple-element.16) | copy-start | bytes 786436
  58.5 4.7 %copy-start.2 = (bf16[2,512,128]{2,1,0:T(8,128)(2,1)S(1)}, bf16[2,512,128]{2,1,0:T(8,128)(2,1)}, u32[]{:S(2)}) copy-start(bf16[2,512,128]{2,1,0:T(8,128)(2,1)} %get-tuple-element.17) | copy-start | bytes 786436

commit v2 on v1

v2 whole, which is shorter than its diff:
```python
import jax
import jax.numpy as jnp
from jax import lax
from jax.experimental import pallas as pl
from jax.experimental.pallas import tpu as pltpu
from jax.sharding import PartitionSpec as P

MESH = pl.DeviceIdType.MESH
F32 = jnp.float32
BF16 = jnp.bfloat16
CLIP = 0.5
C = 128
POS = 4
DIRS = [(dx, dy) for dx in (-1, 0, 1) for dy in (-1, 0, 1) if (dx, dy) != (0, 0)]
ORDERS = [(0, 1, 2), (1, 2, 0), (2, 0, 1)]
NT = (((1,), (1,)), ((), ()))


def span(d, size, halo):
    if d == 0:
        return pl.ds(1, 16)
    if d < 0:
        return pl.ds(0 if halo else 1, 1)
    return pl.ds(17 if halo else 16, 1)


def step_kernel(
    pos_ref, gain_ref, feat_hbm, cot_hbm, k1_hbm, k2_hbm,
    outv, full_ref, stats_ref,
    feat, cot, w1, w2, r1, r2, r2y, grid1, land, grid2, ag, au, ah, ap, pre_ref, hg_ref,
    hid, pgr, part, rcore, sa, ra, sb, rb, rc, gains, units, invs,
    in_sem, hs, hr, cs, cr, a_s, a_r, b_s, b_r, c_s, c_r, eb_s, eb_r, ea_s, ea_r, sib_s, sib_r, gs, gr,
):
    gx = lax.axis_index("gx")
    gy = lax.axis_index("gy")
    core = gy % 2
    coord = ((gy // 2) % 2 * 2 + gx // 4, gx % 4, gy // 4)

    def device(x, y, z):
        return (x % 2 * 4 + y, z * 4 + x // 2 * 2 + core)

    def peer(axis, value):
        return device(*(value if i == axis else coord[i] for i in range(3)))

    sibling = (gx, gy + 1 - 2 * core)

    def there(d):
        x, y = gx + d[0], gy + d[1]
        return (x >= 0) & (x < 8) & (y >= 0) & (y < 16)

    def load(i, src, dst):
        return pltpu.make_async_copy(src, dst, in_sem.at[i])

    loads = [load(0, feat_hbm, feat), load(1, cot_hbm, cot), load(2, k1_hbm, w1), load(3, k2_hbm, w2)]
    for c in loads:
        c.start()

    for g in (grid1, land, grid2):
        for f in range(2):
            for e in (0, 17):
                g[f, e] = jnp.zeros((18, 8, C), BF16)
                for x in range(1, 17):
                    g[f, x, e] = jnp.zeros((8, C), BF16)

    barrier = pltpu.get_barrier_semaphore()
    for d in DIRS:
        @pl.when(there(d))
        def _():
            pl.semaphore_signal(barrier, inc=1, device_id=(gx + d[0], gy + d[1]), device_id_type=MESH)
    for axis in range(3):
        for k in (1, 2, 3):
            pl.semaphore_signal(barrier, inc=1, device_id=peer(axis, (coord[axis] + k) % 4), device_id_type=MESH)
    pl.semaphore_signal(barrier, inc=1, device_id=sibling, device_id_type=MESH)

    p0, p1 = pos_ref[0], pos_ref[1]
    where = [jnp.minimum(p0, POS - 1), jnp.minimum(p1, POS - 1)]
    bx = [w // 2 for w in where]
    by = [w % 2 for w in where]
    live = [(p0 < POS).astype(F32), (p1 < POS).astype(F32)]

    def place(grid, f, source):
        for p in range(POS):
            m0, m1 = (p0 == p).astype(F32), (p1 == p).astype(F32)
            for x in range(8):
                rows = pl.ds(x * 64, 64)
                v = source[0, rows].astype(F32) * m0 + source[1, rows].astype(F32) * m1
                grid[f, 1 + p // 2 * 8 + x, pl.ds(1 + p % 2 * 8, 8)] = v.reshape(8, 8, C).astype(BF16)

    def halo(phase, grid, landing):
        def copies(d):
            i = DIRS.index(d)
            return pltpu.make_async_remote_copy(
                src_ref=grid.at[:, span(d[0], 16, False), span(d[1], 16, False)],
                dst_ref=landing.at[:, span(-d[0], 16, True), span(-d[1], 16, True)],
                send_sem=hs.at[phase, i], recv_sem=hr.at[phase, i],
                device_id=(gx + d[0], gy + d[1]), device_id_type=MESH,
            )

        def start():
            for d in DIRS:
                @pl.when(there(d))
                def _():
                    copies(d).start()

        def arrive():
            for d in DIRS:
                @pl.when(there((-d[0], -d[1])))
                def _():
                    copies(d).wait_recv()

        def done():
            for d in DIRS:
                @pl.when(there(d))
                def _():
                    copies(d).wait_send()

        return start, arrive, done

    start1, arrive1, done1 = halo(0, grid1, land)
    start2, arrive2, done2 = halo(1, grid2, grid2)

    loads[0].wait()
    loads[1].wait()
    place(grid1, 0, feat)
    place(grid1, 1, cot)

    expected = 10
    for d in DIRS:
        expected = expected + there(d).astype(jnp.int32)
    pl.semaphore_wait(barrier, expected)
    start1()

    loads[2].wait()
    loads[3].wait()
    for w, r in ((w2, r2), (w1, r1)):
        for t in range(27):
            r[t // 9, :, pl.ds(t % 9 * C, C)] = w[26 - t]
    for t in range(27):
        r2y[t // 9, t % 9 // 3, :, pl.ds(t % 3 * C, C)] = w2[26 - t]

    z = lax.broadcasted_iota(jnp.int32, (10, 8, C), 1)
    first, last = z == 0, z == 7

    def gather(a, s, grid, f):
        def layer(x, carry):
            t = grid[f, bx[s] * 8 + x, pl.ds(by[s] * 8, 10)].astype(F32)
            down = jnp.where(first, 0.0, pltpu.roll(t, 1, 1))
            up = jnp.where(last, 0.0, pltpu.roll(t, 7, 1))
            for oz, v in enumerate((down, t, up)):
                for oy in range(3):
                    a[s, x, :, pl.ds((oy * 3 + oz) * C, C)] = (
                        v[oy : oy + 8].reshape(64, C).astype(BF16)
                    )
            return carry

        lax.fori_loop(0, 10, layer, 0)

    def conv(a, s, w):
        total = None
        for ox in range(3):
            v = jnp.dot(a[s, pl.ds(ox, 8)].reshape(512, 9 * C), w[pl.ds(ox * 9, 9)].reshape(9 * C, C), preferred_element_type=F32)
            total = v if total is None else total + v
        return total

    def conv_t(a, s, r):
        total = None
        for ox in range(3):
            v = lax.dot_general(a[s, pl.ds(ox, 8)].reshape(512, 9 * C), r[ox], NT, preferred_element_type=F32)
            total = v if total is None else total + v
        return total

    def fix(a, s, f, total, weights, block):
        cx = weights(a[s, bx[s] * 9], bx[s] * 2)
        for i in (0, 1):
            edge = (bx[s] == i).astype(F32)
            total[s, i * 7] = total[s, i * 7] + (cx * edge).reshape(8, 8, C)
        t = grid1[f, pl.ds(bx[s] * 8, 10), by[s] * 17].astype(F32)
        layer = lax.broadcasted_iota(jnp.int32, (10, 8, C), 0)
        low, high = (bx[s] == 1).astype(F32), (bx[s] == 0).astype(F32)
        t = t * jnp.where(layer == 0, low, jnp.where(layer == 9, high, 1.0))
        down = jnp.where(first, 0.0, pltpu.roll(t, 1, 1))
        up = jnp.where(last, 0.0, pltpu.roll(t, 7, 1))
        cy = None
        for ox in range(3):
            rows = jnp.concatenate([v[ox : ox + 8].reshape(64, C) for v in (down, t, up)], axis=1).astype(BF16)
            v = block(rows, ox, by[s] * 2)
            cy = v if cy is None else cy + v
        for i in (0, 1):
            edge = (by[s] == i).astype(F32)
            total[s, :, i * 7] = total[s, :, i * 7] + (cy * edge).reshape(8, 8, C)

    def fix_first(s):
        fix(ag, s, 0, pre_ref,
            lambda rows, ox: jnp.dot(rows, w1[pl.ds(ox * 9, 9)].reshape(9 * C, C), preferred_element_type=F32),
            lambda rows, ox, oy: jnp.dot(
                rows, w1[pl.ds(ox * 9 + oy * 3, 3)].reshape(3 * C, C), preferred_element_type=F32))

    def fix_second(s):
        fix(au, s, 1, hg_ref,
            lambda rows, ox: lax.dot_general(rows, r2[ox], NT, preferred_element_type=F32),
            lambda rows, ox, oy: lax.dot_general(
                rows, r2y[ox, oy], NT, preferred_element_type=F32))

    for s in range(2):
        gather(ag, s, grid1, 0)
        pre_ref[s] = conv(ag, s, w1).reshape(8, 8, 8, C)
    for s in range(2):
        gather(au, s, grid1, 1)
        hg_ref[s] = conv_t(au, s, r2).reshape(8, 8, 8, C)

    arrive1()
    for f in range(2):
        for e in (0, 17):
            grid1[f, e] = land[f, e]
            for x in range(1, 17):
                grid1[f, x, e] = land[f, x, e]
    gain = gain_ref[0:1, :]

    half = pl.multiple_of(core * 64, 64)
    other = pl.multiple_of((1 - core) * 64, 64)

    def core_copy(g):
        return pltpu.make_async_remote_copy(
            src_ref=part.at[pl.ds(g * 9, 9), pl.ds(other, 64)], dst_ref=rcore.at[pl.ds(g * 9, 9)],
            send_sem=cs.at[g], recv_sem=cr.at[g], device_id=sibling, device_id_type=MESH)

    def group(g, a, lhs):
        ox = 2 - g if g < 3 else g - 3
        v = (jnp.dot(lhs[0], a[0, pl.ds(ox, 8)].reshape(512, 9 * C), preferred_element_type=F32)
             + jnp.dot(lhs[1], a[1, pl.ds(ox, 8)].reshape(512, 9 * C), preferred_element_type=F32))
        for k in range(9):
            if g < 3:
                part[g * 9 + 8 - k] = v[:, k * C : (k + 1) * C]
            else:
                part[g * 9 + k] = v[:, k * C : (k + 1) * C].T
        core_copy(g).start()

    def axes(g):
        return ORDERS[g % 3]

    def remote(src, dst, send_sem, recv_sem, to):
        return pltpu.make_async_remote_copy(
            src_ref=src, dst_ref=dst, send_sem=send_sem, recv_sem=recv_sem, device_id=to, device_id_type=MESH)

    def local(ref, send_sem, recv_sem):
        return remote(ref, ref, send_sem, recv_sem, sibling)

    def three(axis, copy):
        for k in (1, 2, 3):
            to = (coord[axis] + k) % 4
            copy(k - 1, to, peer(axis, to)).start()

    def all_a(g):
        return local(ra.at[g], a_s.at[g], a_r.at[g])

    def all_b(g):
        return local(rb.at[g], b_s.at[g], b_r.at[g])

    def all_c(g):
        return local(rc.at[g, pl.ds(0, 3)], c_s.at[g], c_r.at[g])

    def all_eb(g):
        return local(full_ref.at[g, 0, 0, pl.ds(0, 15)], eb_s.at[g], eb_r.at[g])

    def all_ea(g):
        return local(full_ref.at[g, 0, pl.ds(0, 3)], ea_s.at[g], ea_r.at[g])

    def scatter(g):
        core_copy(g).wait_recv()

        def tap(k, carry):
            v = part[g * 9 + k, pl.ds(half, 64)] + rcore[g * 9 + k]
            rcore[g * 9 + k] = v
            sa[g, k] = v.reshape(4, 16, C).astype(BF16)
            return carry

        lax.fori_loop(0, 9, tap, 0)
        three(axes(g)[0], lambda k, to, d: remote(
            sa.at[g, :, to], ra.at[g, k], a_s.at[g], a_r.at[g], d))

    def reduce_a(g):
        all_a(g).wait_recv()
        a, b, _ = axes(g)
        v = rcore[pl.ds(g * 9, 9), pl.ds(pl.multiple_of(coord[a] * 16, 16), 16)]
        for k in range(3):
            v = v + ra[g, k].astype(F32)
        sb[g, pl.ds(0, 18)] = v.reshape(18, 8, C)
        three(b, lambda k, to, d: remote(
            sb.at[g, pl.ds(to * 5, 5)], rb.at[g, k], b_s.at[g], b_r.at[g], d))

    def reduce_b(g):
        all_b(g).wait_recv()
        _, b, c = axes(g)
        v = sb[g, pl.ds(coord[b] * 5, 5)]
        for k in range(3):
            v = v + rb[g, k]
        rc[g, coord[c]] = v
        mine = rc.at[g, coord[c]]
        three(c, lambda k, to, d: remote(mine, mine, c_s.at[g], c_r.at[g], d))

    def reduce_c(g):
        all_c(g).wait_recv()
        a, b, _ = axes(g)
        v = ((rc[g, 0] + rc[g, 1]) + rc[g, 2]) + rc[g, 3]
        full_ref[g, core, coord[a], pl.ds(coord[b] * 5, 5)] = v.astype(BF16)
        mine = full_ref.at[g, core, coord[a], pl.ds(coord[b] * 5, 5)]
        three(b, lambda k, to, d: remote(mine, mine, eb_s.at[g], eb_r.at[g], d))

    def spread(g):
        all_eb(g).wait_recv()
        a = axes(g)[0]
        mine = full_ref.at[g, core, coord[a]]
        three(a, lambda k, to, d: remote(mine, mine, ea_s.at[g], ea_r.at[g], d))

    def sib_copy(chunk):
        ref = full_ref.at[pl.ds(chunk * 3, 3), core]
        return remote(ref, ref, sib_s.at[chunk], sib_r.at[chunk], sibling)

    def pass_on(chunk):
        for g in range(chunk * 3, chunk * 3 + 3):
            all_ea(g).wait_recv()
        sib_copy(chunk).start()

    def gain_copy(stage, k):
        if stage == 0:
            return pltpu.make_async_remote_copy(
                src_ref=gains.at[0, 0], dst_ref=gains.at[0, 1], send_sem=gs.at[0], recv_sem=gr.at[0],
                device_id=sibling, device_id_type=MESH)
        axis = stage - 1
        i = 1 + axis * 3 + k - 1
        return pltpu.make_async_remote_copy(
            src_ref=gains.at[stage, coord[axis]], dst_ref=gains.at[stage, coord[axis]],
            send_sem=gs.at[i], recv_sem=gr.at[i],
            device_id=peer(axis, (coord[axis] + k) % 4), device_id_type=MESH)

    def gain_step(stage):
        if stage == 0:
            gain_copy(0, 0).wait_recv()
            gains[1, coord[0]] = gains[0, 0] + gains[0, 1]
        else:
            for k in (1, 2, 3):
                gain_copy(stage, k).wait_recv()
            v = ((gains[stage, 0] + gains[stage, 1]) + gains[stage, 2]) + gains[stage, 3]
            if stage == 3:
                return v
            gains[stage + 1, coord[stage]] = v
        for k in (1, 2, 3):
            gain_copy(stage + 1, k).start()

    def second_half(s, f):
        if f == 0:
            gather(ah, s, grid2, 0)
            v = conv(ah, s, w2) * live[s] + feat[s].astype(F32) * live[s]
        else:
            gather(ap, s, grid2, 1)
            v = (conv_t(ap, s, r1) + cot[s].astype(F32)) * live[s]
        outv[f, s] = v.astype(BF16)

    def forward(s):
        gather(ag, s, grid1, 0)
        fix_first(s)
        pre = pre_ref[s].reshape(512, C)
        center = pre - jnp.mean(pre, axis=-1, keepdims=True)
        inv = lax.rsqrt(jnp.mean(center * center, axis=-1, keepdims=True) + 1e-05)
        unit = center * inv
        normed = unit * gain
        sig = jax.nn.sigmoid(normed)
        hidden = normed * sig * live[s]
        hid[s] = hidden.astype(BF16)
        units[s] = unit
        invs[s] = jnp.broadcast_to(inv, (512, C))
        return hidden.T.astype(BF16)

    def backward(s):
        fix_second(s)
        hgrad = hg_ref[s].reshape(512, C) * live[s]
        unit, inv = units[s], invs[s]
        normed = unit * gain
        sig = jax.nn.sigmoid(normed)
        dn = hgrad * (sig * (1.0 + normed * (1.0 - sig)))
        du = dn * gain
        dc = inv * (du - unit * jnp.mean(du * unit, axis=-1, keepdims=True))
        pg = (dc - jnp.mean(dc, axis=-1, keepdims=True)) * live[s]
        pgr[s] = pg.astype(BF16)
        return pg.T.astype(BF16), jnp.sum(dn * unit, axis=0, keepdims=True)

    for g in range(6):
        sb[g, pl.ds(18, 2)] = jnp.zeros((2, 8, C), F32)
    hid_t = [forward(0), forward(1)]
    gather(au, 0, grid1, 1)
    gather(au, 1, grid1, 1)
    early, late = (0, 1, 2), (3, 4, 5)
    for g in early:
        group(g, au, hid_t)
    pg0, gg0 = backward(0)
    for g in early:
        scatter(g)
    pg1, gg1 = backward(1)
    gains[0, 0] = jnp.broadcast_to(gg0 + gg1, (8, C))
    gain_copy(0, 0).start()
    for g in late:
        group(g, ag, [pg0, pg1])
    place(grid2, 0, hid)
    place(grid2, 1, pgr)
    start2()
    for g in late:
        scatter(g)
    gain_step(0)
    for g in early:
        reduce_a(g)
    arrive2()
    second_half(0, 0)
    for g in late:
        reduce_a(g)
    for g in early:
        reduce_b(g)
    gain_step(1)
    second_half(1, 0)
    for g in late:
        reduce_b(g)
    for g in early:
        reduce_c(g)
    gain_step(2)
    second_half(0, 1)
    for g in late:
        reduce_c(g)
    for g in early:
        spread(g)
    second_half(1, 1)
    gain_sum = gain_step(3)
    for g in late:
        spread(g)
    pass_on(0)

    def squares(chunk, acc):
        sib_copy(chunk).wait_recv()

        def part_of(i, acc):
            v = full_ref[chunk * 3 + i // 8, i // 4 % 2, i % 4, pl.ds(0, 18)].astype(F32)
            return acc + jnp.sum(v * v, axis=0)

        return lax.fori_loop(0, 24, part_of, acc)

    acc = squares(0, jnp.zeros((8, C), F32))
    pass_on(1)
    acc = squares(1, acc)
    total = jnp.sum(acc) + jnp.sum(gain_sum[0:1] * gain_sum[0:1])
    entries = 54.0 * C * C + C
    mean = jnp.full((8, C), total / entries + 1e-06, F32)
    shrink = jnp.minimum(1.0, CLIP / jnp.sqrt(mean))
    stats_ref[0] = shrink
    stats_ref[1] = shrink * gain_sum

    done1()
    done2()
    for g in range(6):
        core_copy(g).wait_send()
        for sent in (all_a, all_b, all_c, all_eb, all_ea):
            sent(g).wait_send()
    for chunk in (0, 1):
        sib_copy(chunk).wait_send()
    gain_copy(0, 0).wait_send()
    for k in (1, 2, 3):
        for stage in (1, 2, 3):
            gain_copy(stage, k).wait_send()


def finish_kernel(outv, full_ref, stats_ref, out_hbm, fgrad_hbm, update_hbm, gain_ref, scaled, sem):
    copies = [pltpu.make_async_copy(outv.at[0], out_hbm, sem.at[18]),
              pltpu.make_async_copy(outv.at[1], fgrad_hbm, sem.at[19])]
    for c in copies:
        c.start()
    shrink = stats_ref[0, 0:1, :]
    for g in range(6):
        for k in range(9):
            for h in range(2):
                v = full_ref[g, h, :, pl.ds(k * 2, 2)].astype(F32).reshape(64, C)
                scaled[g, k, pl.ds(h * 64, 64)] = v * shrink
            if k % 3 == 2:
                c = pltpu.make_async_copy(
                    scaled.at[g, pl.ds(k - 2, 3)], update_hbm.at[1 - g // 3, pl.ds(g % 3 * 9 + k - 2, 3)],
                    sem.at[g * 3 + k // 3])
                c.start()
                copies.append(c)
    gain_ref[...] = stats_ref[1, 0:1, :]
    for c in copies:
        c.wait()


def per_device(features, brick_pos, cotangent, first_kernel, second_kernel, norm_gain):
    hbm = pl.BlockSpec(memory_space=pltpu.HBM)
    vmem = pl.BlockSpec(memory_space=pltpu.VMEM)
    dma = pltpu.SemaphoreType.DMA
    V = pltpu.VMEM
    tile = (2, 10, 64, 9 * C)
    outv, full, stats = pl.pallas_call(
        step_kernel,
        out_shape=(V((2, 2, 512, C), BF16), V((6, 2, 4, 20, 8, C), BF16), V((2, 8, C), F32)),
        in_specs=[pl.BlockSpec(memory_space=pltpu.SMEM), vmem, hbm, hbm, hbm, hbm],
        out_specs=(vmem, vmem, vmem),
        scratch_shapes=[
            V((2, 512, C), BF16), V((2, 512, C), BF16),
            V((27, C, C), BF16), V((27, C, C), BF16),
            V((3, C, 9 * C), BF16), V((3, C, 9 * C), BF16), V((3, 3, C, 3 * C), BF16),
            V((2, 18, 18, 8, C), BF16), V((2, 18, 18, 8, C), BF16), V((2, 18, 18, 8, C), BF16),
            V(tile, BF16), V(tile, BF16), V(tile, BF16), V(tile, BF16),
            V((2, 8, 8, 8, C), F32), V((2, 8, 8, 8, C), F32),
            V((2, 512, C), BF16), V((2, 512, C), BF16),
            V((54, C, C), F32), V((54, 64, C), F32),
            V((6, 9, 4, 16, C), BF16), V((6, 3, 9, 16, C), BF16),
            V((6, 20, 8, C), F32), V((6, 3, 5, 8, C), F32), V((6, 4, 5, 8, C), F32),
            V((4, 4, 8, C), F32),
            V((2, 512, C), F32), V((2, 512, C), F32),
            dma((4,)), dma((2, 8)), dma((2, 8)), dma((6,)), dma((6,)),
            dma((6,)), dma((6,)), dma((6,)), dma((6,)), dma((6,)), dma((6,)),
            dma((6,)), dma((6,)), dma((6,)), dma((6,)),
            dma((2,)), dma((2,)), dma((10,)), dma((10,)),
        ],
        compiler_params=pltpu.CompilerParams(
            collective_id=0, has_side_effects=True, vmem_limit_bytes=56 * 2**20
        ),
        name="step",
    )(brick_pos, norm_gain.reshape(1, C), features, cotangent, first_kernel, second_kernel)
    out, fgrad, update, gain = pl.pallas_call(
        finish_kernel,
        out_shape=(
            jax.ShapeDtypeStruct((2, 512, C), BF16),
            jax.ShapeDtypeStruct((2, 512, C), BF16),
            jax.ShapeDtypeStruct((2, 27, C, C), F32),
            jax.ShapeDtypeStruct((1, C), F32),
        ),
        in_specs=[vmem, vmem, vmem],
        out_specs=(hbm, hbm, hbm, vmem),
        scratch_shapes=[V((6, 9, C, C), F32), dma((20,))],
        compiler_params=pltpu.CompilerParams(vmem_limit_bytes=10 * 2**20),
        name="finish",
    )(outv, full, stats)
    return out, fgrad, update, gain.reshape(C)


def solution(mesh):
    rows = P(("gx", "gy"), None, None)
    return jax.shard_map(
        per_device, mesh=mesh, in_specs=(rows, P(("gx", "gy")), rows, P(), P(), P()),
        out_specs=(rows, rows, P(), P()), check_vma=False,
    )
```

time: 64.1 us -> 54.1 us (0.84)
  Pallas kernels: 58.5 us -> 53.3 us
  local copies, waits for them, and re-layouts: 4.76 us -> 0 us
    pallas_call x2, Pallas kernels: 58.5 us -> 53.3 us  [the longest x1 50.7 us: per_device(): pl.pallas_call(step_kernel, out_shape=(V((2, 2, 512, C), BF16), V((6, 2,...]
    unnamed x10 -> x0, local copies, waits for them, and re-layouts: 3.58 us -> none
    squeeze x1 -> x0, local copies, waits for them, and re-layouts: 1.18 us -> none  [per_device(): return (out, fgrad, update.reshape(2, 27, C, C), stats[1, 0])]
where the time goes in v2:
time: 54.1 us; the launch traced here: 54 us
  Pallas kernels  53.3 us (99%)
  between operations  0.64 us (1%)
    pallas_call x1, Pallas kernels, per_device(): pl.pallas_call(step_kernel, out_shape=(V((2, 2, 512, C), BF16), V((6, 2,...  50.7 us
    pallas_call x1, Pallas kernels, per_device(): pl.pallas_call(finish_kernel, out_shape=(jax.ShapeDtypeStruct((2, 512, C)...  2.63 us

profile of v2, /device:TPU:1, one launch (start us, length us, event | category | flops | bytes accessed | tf_op | source)
XLA Modules:
  0.0 54.0 jit_solution(15343109318147193341)
XLA Ops:
  0.6 50.7 %step.1 = (bf16[2,2,512,128]{3,2,1,0:T(8,128)(2,1)S(1)}, bf16[6,2,4,20,8,128]{5,4,3,2,1,0:T(8,128)(2,1)S(1)}, f32[2,8,128]{2,1,0:T(8,128)S(1)}) custom-call(s32[2]{0:T(128)} %pos_ref.1, f32[1,128]{1,0:T(1,128)} %bitcast.2, bf16[2,512,128]{2,1,0:T(8,128)(2,1)} %feat_hbm.1, bf16[2,512,128]{2,1,0:T(8,128)(2,1)} %cot_hbm.1, bf16[27,128,128]{2,1,0:T(8,128)(2,1)} %k1_hbm.1, ...), custom_call_target="tpu_custom_call" | custom-call | tf_op jit(solution)/shard_map/step/pallas_call | solution.py:496
  51.3 2.6 %finish.1 = (bf16[2,512,128]{2,1,0:T(8,128)(2,1)}, bf16[2,512,128]{2,1,0:T(8,128)(2,1)}, f32[2,27,128,128]{3,2,1,0:T(8,128)}, f32[1,128]{1,0:T(1,128)}) custom-call(bf16[2,2,512,128]{3,2,1,0:T(8,128)(2,1)S(1)} %get-tuple-element.11.outv, bf16[6,2,4,20,8,128]{5,4,3,2,1,0:T(8,128)(2,1)S(1)} %get-tuple-element.12.full_ref, ...), custom_call_target="tpu_custom_call" | custom-call | tf_op jit(solution)/shard_map/finish/pallas_call | solution.py:524

commit v3 on v2

--- a/solution.py
+++ b/solution.py
@@ -132,28 +132,42 @@
 
     loads[2].wait()
     loads[3].wait()
-    for w, r in ((w2, r2), (w1, r1)):
-        for t in range(27):
-            r[t // 9, :, pl.ds(t % 9 * C, C)] = w[26 - t]
     for t in range(27):
+        r2[t // 9, :, pl.ds(t % 9 * C, C)] = w2[26 - t]
         r2y[t // 9, t % 9 // 3, :, pl.ds(t % 3 * C, C)] = w2[26 - t]
 
     z = lax.broadcasted_iota(jnp.int32, (10, 8, C), 1)
     first, last = z == 0, z == 7
 
-    def gather(a, s, grid, f):
+    def sides(t):
+        n = t.shape[0]
+        return (jnp.where(first[:n], 0.0, pltpu.roll(t, 1, 1)), t, jnp.where(last[:n], 0.0, pltpu.roll(t, 7, 1)))
+
+    def gather(a, s, grid, f, layers=None):
         def layer(x, carry):
             t = grid[f, bx[s] * 8 + x, pl.ds(by[s] * 8, 10)].astype(F32)
-            down = jnp.where(first, 0.0, pltpu.roll(t, 1, 1))
-            up = jnp.where(last, 0.0, pltpu.roll(t, 7, 1))
-            for oz, v in enumerate((down, t, up)):
+            for oz, v in enumerate(sides(t)):
                 for oy in range(3):
-                    a[s, x, :, pl.ds((oy * 3 + oz) * C, C)] = (
-                        v[oy : oy + 8].reshape(64, C).astype(BF16)
-                    )
+                    a[s, x, :, pl.ds((oy * 3 + oz) * C, C)] = v[oy : oy + 8].reshape(64, C).astype(BF16)
             return carry
 
-        lax.fori_loop(0, 10, layer, 0)
+        if layers is None:
+            lax.fori_loop(0, 10, layer, 0)
+        else:
+            for x in layers:
+                layer(x, 0)
+
+    def patch(a, s, grid, f):
+        gather(a, s, grid, f, (0, 9))
+
+        def layer(x, carry):
+            for oy in (0, 2):
+                t = grid[f, bx[s] * 8 + x, pl.ds(by[s] * 8 + oy * 4, 2)].astype(F32)
+                for oz, v in enumerate(sides(t)):
+                    a[s, x, pl.ds(oy * 24, 16), pl.ds((oy * 3 + oz) * C, C)] = v.reshape(16, C).astype(BF16)
+            return carry
+
+        lax.fori_loop(1, 9, layer, 0)
 
     def conv(a, s, w):
         total = None
@@ -173,30 +187,29 @@
         cx = weights(a[s, bx[s] * 9], bx[s] * 2)
         for i in (0, 1):
             edge = (bx[s] == i).astype(F32)
-            total[s, i * 7] = total[s, i * 7] + (cx * edge).reshape(8, 8, C)
+            total[i * 7] = total[i * 7] + (cx * edge).reshape(8, 8, C)
         t = grid1[f, pl.ds(bx[s] * 8, 10), by[s] * 17].astype(F32)
         layer = lax.broadcasted_iota(jnp.int32, (10, 8, C), 0)
         low, high = (bx[s] == 1).astype(F32), (bx[s] == 0).astype(F32)
         t = t * jnp.where(layer == 0, low, jnp.where(layer == 9, high, 1.0))
-        down = jnp.where(first, 0.0, pltpu.roll(t, 1, 1))
-        up = jnp.where(last, 0.0, pltpu.roll(t, 7, 1))
+        shifted = sides(t)
         cy = None
         for ox in range(3):
-            rows = jnp.concatenate([v[ox : ox + 8].reshape(64, C) for v in (down, t, up)], axis=1).astype(BF16)
+            rows = jnp.concatenate([v[ox : ox + 8].reshape(64, C) for v in shifted], axis=1).astype(BF16)
             v = block(rows, ox, by[s] * 2)
             cy = v if cy is None else cy + v
         for i in (0, 1):
             edge = (by[s] == i).astype(F32)
-            total[s, :, i * 7] = total[s, :, i * 7] + (cy * edge).reshape(8, 8, C)
+            total[:, i * 7] = total[:, i * 7] + (cy * edge).reshape(8, 8, C)
 
     def fix_first(s):
-        fix(ag, s, 0, pre_ref,
+        fix(ag, s, 0, pre_ref.at[s],
             lambda rows, ox: jnp.dot(rows, w1[pl.ds(ox * 9, 9)].reshape(9 * C, C), preferred_element_type=F32),
             lambda rows, ox, oy: jnp.dot(
                 rows, w1[pl.ds(ox * 9 + oy * 3, 3)].reshape(3 * C, C), preferred_element_type=F32))
 
-    def fix_second(s):
-        fix(au, s, 1, hg_ref,
+    def fix_second():
+        fix(au, 0, 1, hg_ref,
             lambda rows, ox: lax.dot_general(rows, r2[ox], NT, preferred_element_type=F32),
             lambda rows, ox, oy: lax.dot_general(
                 rows, r2y[ox, oy], NT, preferred_element_type=F32))
@@ -204,9 +217,8 @@
     for s in range(2):
         gather(ag, s, grid1, 0)
         pre_ref[s] = conv(ag, s, w1).reshape(8, 8, 8, C)
-    for s in range(2):
-        gather(au, s, grid1, 1)
-        hg_ref[s] = conv_t(au, s, r2).reshape(8, 8, 8, C)
+    gather(au, 0, grid1, 1)
+    hg_ref[...] = conv_t(au, 0, r2).reshape(8, 8, 8, C)
 
     arrive1()
     for f in range(2):
@@ -312,14 +324,31 @@
         mine = full_ref.at[g, core, coord[a]]
         three(a, lambda k, to, d: remote(mine, mine, ea_s.at[g], ea_r.at[g], d))
 
-    def sib_copy(chunk):
-        ref = full_ref.at[pl.ds(chunk * 3, 3), core]
-        return remote(ref, ref, sib_s.at[chunk], sib_r.at[chunk], sibling)
-
-    def pass_on(chunk):
-        for g in range(chunk * 3, chunk * 3 + 3):
-            all_ea(g).wait_recv()
-        sib_copy(chunk).start()
+    def sib_copy(g):
+        ref = full_ref.at[g, core]
+        return remote(ref, ref, sib_s.at[g], sib_r.at[g], sibling)
+
+    def squares(g, h):
+        acc = None
+        for a in range(4):
+            v = full_ref[g, h, a, pl.ds(0, 18)].astype(F32)
+            v = jnp.sum(v * v, axis=0)
+            acc = v if acc is None else acc + v
+        return acc
+
+    def pass_on(g):
+        all_ea(g).wait_recv()
+        sib_copy(g).start()
+
+    def close(groups):
+        for g in groups:
+            pass_on(g)
+        own = [squares(g, core) for g in groups]
+        acc = jnp.zeros((8, C), F32)
+        for g, mine in zip(groups, own):
+            sib_copy(g).wait_recv()
+            acc = acc + (mine + squares(g, 1 - core))
+        return acc
 
     def gain_copy(stage, k):
         if stage == 0:
@@ -357,7 +386,7 @@
         outv[f, s] = v.astype(BF16)
 
     def forward(s):
-        gather(ag, s, grid1, 0)
+        patch(ag, s, grid1, 0)
         fix_first(s)
         pre = pre_ref[s].reshape(512, C)
         center = pre - jnp.mean(pre, axis=-1, keepdims=True)
@@ -372,8 +401,11 @@
         return hidden.T.astype(BF16)
 
     def backward(s):
-        fix_second(s)
-        hgrad = hg_ref[s].reshape(512, C) * live[s]
+        if s == 0:
+            fix_second()
+            hgrad = hg_ref[...].reshape(512, C) * live[s]
+        else:
+            hgrad = conv_t(au, s, r2) * live[s]
         unit, inv = units[s], invs[s]
         normed = unit * gain
         sig = jax.nn.sigmoid(normed)
@@ -387,7 +419,7 @@
     for g in range(6):
         sb[g, pl.ds(18, 2)] = jnp.zeros((2, 8, C), F32)
     hid_t = [forward(0), forward(1)]
-    gather(au, 0, grid1, 1)
+    patch(au, 0, grid1, 1)
     gather(au, 1, grid1, 1)
     early, late = (0, 1, 2), (3, 4, 5)
     for g in early:
@@ -400,12 +432,15 @@
     gain_copy(0, 0).start()
     for g in late:
         group(g, ag, [pg0, pg1])
+    scatter(3)
+    scatter(4)
     place(grid2, 0, hid)
+    scatter(5)
     place(grid2, 1, pgr)
     start2()
-    for g in late:
-        scatter(g)
     gain_step(0)
+    for t in range(27):
+        r1[t // 9, :, pl.ds(t % 9 * C, C)] = w1[26 - t]
     for g in early:
         reduce_a(g)
     arrive2()
@@ -430,20 +465,9 @@
     gain_sum = gain_step(3)
     for g in late:
         spread(g)
-    pass_on(0)
-
-    def squares(chunk, acc):
-        sib_copy(chunk).wait_recv()
-
-        def part_of(i, acc):
-            v = full_ref[chunk * 3 + i // 8, i // 4 % 2, i % 4, pl.ds(0, 18)].astype(F32)
-            return acc + jnp.sum(v * v, axis=0)
-
-        return lax.fori_loop(0, 24, part_of, acc)
-
-    acc = squares(0, jnp.zeros((8, C), F32))
-    pass_on(1)
-    acc = squares(1, acc)
+    acc = close(early)
+
+    acc = acc + close(late)
     total = jnp.sum(acc) + jnp.sum(gain_sum[0:1] * gain_sum[0:1])
     entries = 54.0 * C * C + C
     mean = jnp.full((8, C), total / entries + 1e-06, F32)
@@ -455,10 +479,9 @@
     done2()
     for g in range(6):
         core_copy(g).wait_send()
+        sib_copy(g).wait_send()
         for sent in (all_a, all_b, all_c, all_eb, all_ea):
             sent(g).wait_send()
-    for chunk in (0, 1):
-        sib_copy(chunk).wait_send()
     gain_copy(0, 0).wait_send()
     for k in (1, 2, 3):
         for stage in (1, 2, 3):
@@ -504,7 +527,7 @@
             V((3, C, 9 * C), BF16), V((3, C, 9 * C), BF16), V((3, 3, C, 3 * C), BF16),
             V((2, 18, 18, 8, C), BF16), V((2, 18, 18, 8, C), BF16), V((2, 18, 18, 8, C), BF16),
             V(tile, BF16), V(tile, BF16), V(tile, BF16), V(tile, BF16),
-            V((2, 8, 8, 8, C), F32), V((2, 8, 8, 8, C), F32),
+            V((2, 8, 8, 8, C), F32), V((8, 8, 8, C), F32),
             V((2, 512, C), BF16), V((2, 512, C), BF16),
             V((54, C, C), F32), V((54, 64, C), F32),
             V((6, 9, 4, 16, C), BF16), V((6, 3, 9, 16, C), BF16),
@@ -514,7 +537,7 @@
             dma((4,)), dma((2, 8)), dma((2, 8)), dma((6,)), dma((6,)),
             dma((6,)), dma((6,)), dma((6,)), dma((6,)), dma((6,)), dma((6,)),
             dma((6,)), dma((6,)), dma((6,)), dma((6,)),
-            dma((2,)), dma((2,)), dma((10,)), dma((10,)),
+            dma((6,)), dma((6,)), dma((10,)), dma((10,)),
         ],
         compiler_params=pltpu.CompilerParams(
             collective_id=0, has_side_effects=True, vmem_limit_bytes=56 * 2**20

time: 54.1 us -> 54.8 us (1.013)
  Pallas kernels: 53.3 us -> 54.1 us
    pallas_call x1, Pallas kernels: 50.7 us -> 51.4 us  [per_device(): pl.pallas_call(step_kernel, out_shape=(V((2, 2, 512, C), BF16), V((6, 2,...]
where the time goes in v3:
time: 54.8 us; the launch traced here: 54.7 us
  Pallas kernels  54.1 us (99%)
  between operations  0.64 us (1%)
    pallas_call x1, Pallas kernels, per_device(): pl.pallas_call(step_kernel, out_shape=(V((2, 2, 512, C), BF16), V((6, 2,...  51.4 us
    pallas_call x1, Pallas kernels, per_device(): pl.pallas_call(finish_kernel, out_shape=(jax.ShapeDtypeStruct((2, 512, C)...  2.63 us

profile of v3, /device:TPU:1, one launch (start us, length us, event | category | flops | bytes accessed | tf_op | source)
XLA Modules:
  0.0 54.7 jit_solution(14493880599727484469)
XLA Ops:
  0.6 51.4 %step.1 = (bf16[2,2,512,128]{3,2,1,0:T(8,128)(2,1)S(1)}, bf16[6,2,4,20,8,128]{5,4,3,2,1,0:T(8,128)(2,1)S(1)}, f32[2,8,128]{2,1,0:T(8,128)S(1)}) custom-call(s32[2]{0:T(128)} %pos_ref.1, f32[1,128]{1,0:T(1,128)} %bitcast.2, bf16[2,512,128]{2,1,0:T(8,128)(2,1)} %feat_hbm.1, bf16[2,512,128]{2,1,0:T(8,128)(2,1)} %cot_hbm.1, bf16[27,128,128]{2,1,0:T(8,128)(2,1)} %k1_hbm.1, ...), custom_call_target="tpu_custom_call" | custom-call | tf_op jit(solution)/shard_map/step/pallas_call | solution.py:519
  52.1 2.6 %finish.1 = (bf16[2,512,128]{2,1,0:T(8,128)(2,1)}, bf16[2,512,128]{2,1,0:T(8,128)(2,1)}, f32[2,27,128,128]{3,2,1,0:T(8,128)}, f32[1,128]{1,0:T(1,128)}) custom-call(bf16[2,2,512,128]{3,2,1,0:T(8,128)(2,1)S(1)} %get-tuple-element.11.outv, bf16[6,2,4,20,8,128]{5,4,3,2,1,0:T(8,128)(2,1)S(1)} %get-tuple-element.12.full_ref, ...), custom_call_target="tpu_custom_call" | custom-call | tf_op jit(solution)/shard_map/finish/pallas_call | solution.py:547

commit v4 on v3

--- a/solution.py
+++ b/solution.py
@@ -55,13 +55,13 @@
     for c in loads:
         c.start()
 
-    for g in (grid1, land, grid2):
+    def clear(g):
         for f in range(2):
             for e in (0, 17):
                 g[f, e] = jnp.zeros((18, 8, C), BF16)
-                for x in range(1, 17):
-                    g[f, x, e] = jnp.zeros((8, C), BF16)
-
+                g[f, pl.ds(1, 16), e] = jnp.zeros((16, 8, C), BF16)
+
+    clear(land)
     barrier = pltpu.get_barrier_semaphore()
     for d in DIRS:
         @pl.when(there(d))
@@ -72,6 +72,8 @@
             pl.semaphore_signal(barrier, inc=1, device_id=peer(axis, (coord[axis] + k) % 4), device_id_type=MESH)
     pl.semaphore_signal(barrier, inc=1, device_id=sibling, device_id_type=MESH)
 
+    clear(grid1)
+    clear(grid2)
     p0, p1 = pos_ref[0], pos_ref[1]
     where = [jnp.minimum(p0, POS - 1), jnp.minimum(p1, POS - 1)]
     bx = [w // 2 for w in where]
@@ -79,12 +81,13 @@
     live = [(p0 < POS).astype(F32), (p1 < POS).astype(F32)]
 
     def place(grid, f, source):
-        for p in range(POS):
-            m0, m1 = (p0 == p).astype(F32), (p1 == p).astype(F32)
-            for x in range(8):
-                rows = pl.ds(x * 64, 64)
-                v = source[0, rows].astype(F32) * m0 + source[1, rows].astype(F32) * m1
-                grid[f, 1 + p // 2 * 8 + x, pl.ds(1 + p % 2 * 8, 8)] = v.reshape(8, 8, C).astype(BF16)
+        masks = [((p0 == p).astype(F32), (p1 == p).astype(F32)) for p in range(POS)]
+        for x in range(8):
+            rows = pl.ds(x * 64, 64)
+            v0, v1 = source[0, rows].astype(F32), source[1, rows].astype(F32)
+            for p, (m0, m1) in enumerate(masks):
+                v = (v0 * m0 + v1 * m1).reshape(8, 8, C).astype(BF16)
+                grid[f, 1 + p // 2 * 8 + x, pl.ds(1 + p % 2 * 8, 8)] = v
 
     def halo(phase, grid, landing):
         def copies(d):
@@ -224,16 +227,16 @@
     for f in range(2):
         for e in (0, 17):
             grid1[f, e] = land[f, e]
-            for x in range(1, 17):
-                grid1[f, x, e] = land[f, x, e]
+            grid1[f, pl.ds(1, 16), e] = land[f, pl.ds(1, 16), e]
     gain = gain_ref[0:1, :]
 
     half = pl.multiple_of(core * 64, 64)
     other = pl.multiple_of((1 - core) * 64, 64)
 
-    def core_copy(g):
+    def core_copy(g, first=0, count=9):
+        taps = pl.ds(g * 9 + first, count)
         return pltpu.make_async_remote_copy(
-            src_ref=part.at[pl.ds(g * 9, 9), pl.ds(other, 64)], dst_ref=rcore.at[pl.ds(g * 9, 9)],
+            src_ref=part.at[taps, pl.ds(other, 64)], dst_ref=rcore.at[taps],
             send_sem=cs.at[g], recv_sem=cr.at[g], device_id=sibling, device_id_type=MESH)
 
     def group(g, a, lhs):
@@ -245,7 +248,8 @@
                 part[g * 9 + 8 - k] = v[:, k * C : (k + 1) * C]
             else:
                 part[g * 9 + k] = v[:, k * C : (k + 1) * C].T
-        core_copy(g).start()
+            if k % 3 == 2:
+                core_copy(g, 8 - k if g < 3 else k - 2, 3).start()
 
     def axes(g):
         return ORDERS[g % 3]
@@ -432,39 +436,30 @@
     gain_copy(0, 0).start()
     for g in late:
         group(g, ag, [pg0, pg1])
-    scatter(3)
-    scatter(4)
     place(grid2, 0, hid)
-    scatter(5)
+    for g in late:
+        scatter(g)
     place(grid2, 1, pgr)
     start2()
     gain_step(0)
     for t in range(27):
         r1[t // 9, :, pl.ds(t % 9 * C, C)] = w1[26 - t]
-    for g in early:
+    for g in early + late:
         reduce_a(g)
+    gain_step(1)
     arrive2()
     second_half(0, 0)
-    for g in late:
-        reduce_a(g)
-    for g in early:
+    for g in early + late:
         reduce_b(g)
-    gain_step(1)
+    gain_step(2)
     second_half(1, 0)
-    for g in late:
-        reduce_b(g)
-    for g in early:
+    for g in early + late:
         reduce_c(g)
-    gain_step(2)
     second_half(0, 1)
-    for g in late:
-        reduce_c(g)
-    for g in early:
+    for g in early + late:
         spread(g)
+    gain_sum = gain_step(3)
     second_half(1, 1)
-    gain_sum = gain_step(3)
-    for g in late:
-        spread(g)
     acc = close(early)
 
     acc = acc + close(late)

time: 54.8 us -> 52.9 us (0.965)
  Pallas kernels: 54.1 us -> 52 us
    pallas_call x1, Pallas kernels: 51.4 us -> 49.3 us  [per_device(): pl.pallas_call(step_kernel, out_shape=(V((2, 2, 512, C), BF16), V((6, 2,...]
where the time goes in v4:
time: 52.9 us; the launch traced here: 52.8 us
  Pallas kernels  52 us (98%)
  between operations  0.8 us (2%)
    pallas_call x1, Pallas kernels, per_device(): pl.pallas_call(step_kernel, out_shape=(V((2, 2, 512, C), BF16), V((6, 2,...  49.3 us
    pallas_call x1, Pallas kernels, per_device(): pl.pallas_call(finish_kernel, out_shape=(jax.ShapeDtypeStruct((2, 512, C)...  2.63 us

profile of v4, /device:TPU:1, one launch (start us, length us, event | category | flops | bytes accessed | tf_op | source)
XLA Modules:
  0.0 52.8 jit_solution(6925592012460708511)
XLA Ops:
  0.6 49.3 %step.1 = (bf16[2,2,512,128]{3,2,1,0:T(8,128)(2,1)S(1)}, bf16[6,2,4,20,8,128]{5,4,3,2,1,0:T(8,128)(2,1)S(1)}, f32[2,8,128]{2,1,0:T(8,128)S(1)}) custom-call(s32[2]{0:T(128)} %pos_ref.1, f32[1,128]{1,0:T(1,128)} %bitcast.2, bf16[2,512,128]{2,1,0:T(8,128)(2,1)} %feat_hbm.1, bf16[2,512,128]{2,1,0:T(8,128)(2,1)} %cot_hbm.1, bf16[27,128,128]{2,1,0:T(8,128)(2,1)} %k1_hbm.1, ...), custom_call_target="tpu_custom_call" | custom-call | tf_op jit(solution)/shard_map/step/pallas_call | solution.py:514
  50.0 2.6 %finish.1 = (bf16[2,512,128]{2,1,0:T(8,128)(2,1)}, bf16[2,512,128]{2,1,0:T(8,128)(2,1)}, f32[2,27,128,128]{3,2,1,0:T(8,128)}, f32[1,128]{1,0:T(1,128)}) custom-call(bf16[2,2,512,128]{3,2,1,0:T(8,128)(2,1)S(1)} %get-tuple-element.11.outv, bf16[6,2,4,20,8,128]{5,4,3,2,1,0:T(8,128)(2,1)S(1)} %get-tuple-element.12.full_ref, ...), custom_call_target="tpu_custom_call" | custom-call | tf_op jit(solution)/shard_map/finish/pallas_call | solution.py:542

commit v5 on v4

--- a/solution.py
+++ b/solution.py
@@ -27,9 +27,9 @@
 def step_kernel(
     pos_ref, gain_ref, feat_hbm, cot_hbm, k1_hbm, k2_hbm,
     outv, full_ref, stats_ref,
-    feat, cot, w1, w2, r1, r2, r2y, grid1, land, grid2, ag, au, ah, ap, pre_ref, hg_ref,
-    hid, pgr, part, rcore, sa, ra, sb, rb, rc, gains, units, invs,
-    in_sem, hs, hr, cs, cr, a_s, a_r, b_s, b_r, c_s, c_r, eb_s, eb_r, ea_s, ea_r, sib_s, sib_r, gs, gr,
+    feat, cot, w1, w2, r1, r2, grid1, land, grid2, ag, au, ah, ap, pre_ref, hid_t, pgr_t,
+    hid, pgr, part, rcore, sa, ra, sb, rb, rc, gains, sums, units, invs,
+    in_sem, hs, hr, cs, cr, a_s, a_r, b_s, b_r, c_s, c_r, eb_s, eb_r, ea_s, ea_r, sib_s, sib_r, sums_s, sums_r, gs, gr,
 ):
     gx = lax.axis_index("gx")
     gy = lax.axis_index("gy")
@@ -76,8 +76,16 @@
     clear(grid2)
     p0, p1 = pos_ref[0], pos_ref[1]
     where = [jnp.minimum(p0, POS - 1), jnp.minimum(p1, POS - 1)]
-    bx = [w // 2 for w in where]
-    by = [w % 2 for w in where]
+
+    def pick(pair, s):
+        return pair[s] if isinstance(s, int) else jnp.where(s == 0, pair[0], pair[1])
+
+    def bx(s):
+        return pick(where, s) // 2
+
+    def by(s):
+        return pick(where, s) % 2
+
     live = [(p0 < POS).astype(F32), (p1 < POS).astype(F32)]
 
     def place(grid, f, source):
@@ -137,7 +145,6 @@
     loads[3].wait()
     for t in range(27):
         r2[t // 9, :, pl.ds(t % 9 * C, C)] = w2[26 - t]
-        r2y[t // 9, t % 9 // 3, :, pl.ds(t % 3 * C, C)] = w2[26 - t]
 
     z = lax.broadcasted_iota(jnp.int32, (10, 8, C), 1)
     first, last = z == 0, z == 7
@@ -148,7 +155,7 @@
 
     def gather(a, s, grid, f, layers=None):
         def layer(x, carry):
-            t = grid[f, bx[s] * 8 + x, pl.ds(by[s] * 8, 10)].astype(F32)
+            t = grid[f, bx(s) * 8 + x, pl.ds(by(s) * 8, 10)].astype(F32)
             for oz, v in enumerate(sides(t)):
                 for oy in range(3):
                     a[s, x, :, pl.ds((oy * 3 + oz) * C, C)] = v[oy : oy + 8].reshape(64, C).astype(BF16)
@@ -165,7 +172,7 @@
 
         def layer(x, carry):
             for oy in (0, 2):
-                t = grid[f, bx[s] * 8 + x, pl.ds(by[s] * 8 + oy * 4, 2)].astype(F32)
+                t = grid[f, bx(s) * 8 + x, pl.ds(by(s) * 8 + oy * 4, 2)].astype(F32)
                 for oz, v in enumerate(sides(t)):
                     a[s, x, pl.ds(oy * 24, 16), pl.ds((oy * 3 + oz) * C, C)] = v.reshape(16, C).astype(BF16)
             return carry
@@ -187,22 +194,22 @@
         return total
 
     def fix(a, s, f, total, weights, block):
-        cx = weights(a[s, bx[s] * 9], bx[s] * 2)
+        cx = weights(a[s, bx(s) * 9], bx(s) * 2)
         for i in (0, 1):
-            edge = (bx[s] == i).astype(F32)
+            edge = (bx(s) == i).astype(F32)
             total[i * 7] = total[i * 7] + (cx * edge).reshape(8, 8, C)
-        t = grid1[f, pl.ds(bx[s] * 8, 10), by[s] * 17].astype(F32)
+        t = grid1[f, pl.ds(bx(s) * 8, 10), by(s) * 17].astype(F32)
         layer = lax.broadcasted_iota(jnp.int32, (10, 8, C), 0)
-        low, high = (bx[s] == 1).astype(F32), (bx[s] == 0).astype(F32)
+        low, high = (bx(s) == 1).astype(F32), (bx(s) == 0).astype(F32)
         t = t * jnp.where(layer == 0, low, jnp.where(layer == 9, high, 1.0))
         shifted = sides(t)
         cy = None
         for ox in range(3):
             rows = jnp.concatenate([v[ox : ox + 8].reshape(64, C) for v in shifted], axis=1).astype(BF16)
-            v = block(rows, ox, by[s] * 2)
+            v = block(rows, ox, by(s) * 2)
             cy = v if cy is None else cy + v
         for i in (0, 1):
-            edge = (by[s] == i).astype(F32)
+            edge = (by(s) == i).astype(F32)
             total[:, i * 7] = total[:, i * 7] + (cy * edge).reshape(8, 8, C)
 
     def fix_first(s):
@@ -211,18 +218,13 @@
             lambda rows, ox, oy: jnp.dot(
                 rows, w1[pl.ds(ox * 9 + oy * 3, 3)].reshape(3 * C, C), preferred_element_type=F32))
 
-    def fix_second():
-        fix(au, 0, 1, hg_ref,
-            lambda rows, ox: lax.dot_general(rows, r2[ox], NT, preferred_element_type=F32),
-            lambda rows, ox, oy: lax.dot_general(
-                rows, r2y[ox, oy], NT, preferred_element_type=F32))
-
-    for s in range(2):
+    def first_local(s, carry):
         gather(ag, s, grid1, 0)
         pre_ref[s] = conv(ag, s, w1).reshape(8, 8, 8, C)
-    gather(au, 0, grid1, 1)
-    hg_ref[...] = conv_t(au, 0, r2).reshape(8, 8, 8, C)
-
+        gather(au, s, grid1, 1)
+        return carry
+
+    lax.fori_loop(0, 2, first_local, 0)
     arrive1()
     for f in range(2):
         for e in (0, 17):
@@ -239,17 +241,17 @@
             src_ref=part.at[taps, pl.ds(other, 64)], dst_ref=rcore.at[taps],
             send_sem=cs.at[g], recv_sem=cr.at[g], device_id=sibling, device_id_type=MESH)
 
-    def group(g, a, lhs):
-        ox = 2 - g if g < 3 else g - 3
+    def group(g, flip, a, lhs):
+        ox = 2 - g if flip else g - 3
         v = (jnp.dot(lhs[0], a[0, pl.ds(ox, 8)].reshape(512, 9 * C), preferred_element_type=F32)
              + jnp.dot(lhs[1], a[1, pl.ds(ox, 8)].reshape(512, 9 * C), preferred_element_type=F32))
         for k in range(9):
-            if g < 3:
+            if flip:
                 part[g * 9 + 8 - k] = v[:, k * C : (k + 1) * C]
             else:
                 part[g * 9 + k] = v[:, k * C : (k + 1) * C].T
             if k % 3 == 2:
-                core_copy(g, 8 - k if g < 3 else k - 2, 3).start()
+                core_copy(g, 8 - k if flip else k - 2, 3).start()
 
     def axes(g):
         return ORDERS[g % 3]
@@ -262,7 +264,7 @@
         return remote(ref, ref, send_sem, recv_sem, sibling)
 
     def three(axis, copy):
-        for k in (1, 2, 3):
+        for k in (2, 1, 3):
             to = (coord[axis] + k) % 4
             copy(k - 1, to, peer(axis, to)).start()
 
@@ -344,15 +346,14 @@
         all_ea(g).wait_recv()
         sib_copy(g).start()
 
-    def close(groups):
+    def close(groups, acc):
         for g in groups:
             pass_on(g)
-        own = [squares(g, core) for g in groups]
-        acc = jnp.zeros((8, C), F32)
-        for g, mine in zip(groups, own):
-            sib_copy(g).wait_recv()
-            acc = acc + (mine + squares(g, 1 - core))
+        for g in groups:
+            acc = acc + squares(g, core)
         return acc
+
+    sums_copy = remote(sums.at[0], sums.at[1], sums_s.at[0], sums_r.at[0], sibling)
 
     def gain_copy(stage, k):
         if stage == 0:
@@ -380,16 +381,19 @@
         for k in (1, 2, 3):
             gain_copy(stage + 1, k).start()
 
-    def second_half(s, f):
-        if f == 0:
-            gather(ah, s, grid2, 0)
-            v = conv(ah, s, w2) * live[s] + feat[s].astype(F32) * live[s]
-        else:
-            gather(ap, s, grid2, 1)
-            v = (conv_t(ap, s, r1) + cot[s].astype(F32)) * live[s]
-        outv[f, s] = v.astype(BF16)
-
-    def forward(s):
+    def outputs(s, carry):
+        gather(ah, s, grid2, 0)
+        v = conv(ah, s, w2) * pick(live, s) + feat[s].astype(F32) * pick(live, s)
+        outv[0, s] = v.astype(BF16)
+        return carry
+
+    def feature_grads(s, carry):
+        gather(ap, s, grid2, 1)
+        v = (conv_t(ap, s, r1) + cot[s].astype(F32)) * pick(live, s)
+        outv[1, s] = v.astype(BF16)
+        return carry
+
+    def forward(s, carry):
         patch(ag, s, grid1, 0)
         fix_first(s)
         pre = pre_ref[s].reshape(512, C)
@@ -397,72 +401,81 @@
         inv = lax.rsqrt(jnp.mean(center * center, axis=-1, keepdims=True) + 1e-05)
         unit = center * inv
         normed = unit * gain
-        sig = jax.nn.sigmoid(normed)
-        hidden = normed * sig * live[s]
+        hidden = normed * jax.nn.sigmoid(normed) * pick(live, s)
         hid[s] = hidden.astype(BF16)
         units[s] = unit
         invs[s] = jnp.broadcast_to(inv, (512, C))
-        return hidden.T.astype(BF16)
-
-    def backward(s):
-        if s == 0:
-            fix_second()
-            hgrad = hg_ref[...].reshape(512, C) * live[s]
-        else:
-            hgrad = conv_t(au, s, r2) * live[s]
+        hid_t[s] = hidden.T.astype(BF16)
+        patch(au, s, grid1, 1)
+        return carry
+
+    def backward(s, total):
+        hgrad = conv_t(au, s, r2) * pick(live, s)
         unit, inv = units[s], invs[s]
         normed = unit * gain
         sig = jax.nn.sigmoid(normed)
         dn = hgrad * (sig * (1.0 + normed * (1.0 - sig)))
         du = dn * gain
         dc = inv * (du - unit * jnp.mean(du * unit, axis=-1, keepdims=True))
-        pg = (dc - jnp.mean(dc, axis=-1, keepdims=True)) * live[s]
+        pg = (dc - jnp.mean(dc, axis=-1, keepdims=True)) * pick(live, s)
         pgr[s] = pg.astype(BF16)
-        return pg.T.astype(BF16), jnp.sum(dn * unit, axis=0, keepdims=True)
+        pgr_t[s] = pg.T.astype(BF16)
+        return total + jnp.sum(dn * unit, axis=0, keepdims=True)
 
     for g in range(6):
         sb[g, pl.ds(18, 2)] = jnp.zeros((2, 8, C), F32)
-    hid_t = [forward(0), forward(1)]
-    patch(au, 0, grid1, 1)
-    gather(au, 1, grid1, 1)
+    lax.fori_loop(0, 2, forward, 0)
     early, late = (0, 1, 2), (3, 4, 5)
-    for g in early:
-        group(g, au, hid_t)
-    pg0, gg0 = backward(0)
+
+    def early_group(g, carry):
+        group(g, True, au, hid_t)
+        return carry
+
+    def late_group(g, carry):
+        group(g, False, ag, pgr_t)
+        return carry
+
+    lax.fori_loop(0, 3, early_group, 0)
+    gsum = lax.fori_loop(0, 2, backward, jnp.zeros((1, C), F32))
     for g in early:
         scatter(g)
-    pg1, gg1 = backward(1)
-    gains[0, 0] = jnp.broadcast_to(gg0 + gg1, (8, C))
+    gains[0, 0] = jnp.broadcast_to(gsum, (8, C))
     gain_copy(0, 0).start()
-    for g in late:
-        group(g, ag, [pg0, pg1])
+    lax.fori_loop(3, 6, late_group, 0)
     place(grid2, 0, hid)
+    place(grid2, 1, pgr)
+    start2()
     for g in late:
         scatter(g)
-    place(grid2, 1, pgr)
-    start2()
     gain_step(0)
     for t in range(27):
         r1[t // 9, :, pl.ds(t % 9 * C, C)] = w1[26 - t]
-    for g in early + late:
+    for g in early:
+        reduce_a(g)
+    arrive2()
+    for g in late:
         reduce_a(g)
     gain_step(1)
-    arrive2()
-    second_half(0, 0)
     for g in early + late:
         reduce_b(g)
+    lax.fori_loop(0, 2, outputs, 0)
     gain_step(2)
-    second_half(1, 0)
     for g in early + late:
         reduce_c(g)
-    second_half(0, 1)
-    for g in early + late:
+    lax.fori_loop(0, 2, feature_grads, 0)
+    for g in early:
+        spread(g)
+    for g in late:
         spread(g)
     gain_sum = gain_step(3)
-    second_half(1, 1)
-    acc = close(early)
-
-    acc = acc + close(late)
+    acc = close(early, jnp.zeros((8, C), F32))
+    acc = close(late, acc)
+    sums[0] = acc
+    sums_copy.start()
+    for g in early + late:
+        sib_copy(g).wait_recv()
+    sums_copy.wait_recv()
+    acc = acc + sums[1]
     total = jnp.sum(acc) + jnp.sum(gain_sum[0:1] * gain_sum[0:1])
     entries = 54.0 * C * C + C
     mean = jnp.full((8, C), total / entries + 1e-06, F32)
@@ -478,6 +491,7 @@
         for sent in (all_a, all_b, all_c, all_eb, all_ea):
             sent(g).wait_send()
     gain_copy(0, 0).wait_send()
+    sums_copy.wait_send()
     for k in (1, 2, 3):
         for stage in (1, 2, 3):
             gain_copy(stage, k).wait_send()
@@ -519,20 +533,20 @@
         scratch_shapes=[
             V((2, 512, C), BF16), V((2, 512, C), BF16),
             V((27, C, C), BF16), V((27, C, C), BF16),
-            V((3, C, 9 * C), BF16), V((3, C, 9 * C), BF16), V((3, 3, C, 3 * C), BF16),
+            V((3, C, 9 * C), BF16), V((3, C, 9 * C), BF16),
             V((2, 18, 18, 8, C), BF16), V((2, 18, 18, 8, C), BF16), V((2, 18, 18, 8, C), BF16),
             V(tile, BF16), V(tile, BF16), V(tile, BF16), V(tile, BF16),
-            V((2, 8, 8, 8, C), F32), V((8, 8, 8, C), F32),
+            V((2, 8, 8, 8, C), F32), V((2, C, 512), BF16), V((2, C, 512), BF16),
             V((2, 512, C), BF16), V((2, 512, C), BF16),
             V((54, C, C), F32), V((54, 64, C), F32),
             V((6, 9, 4, 16, C), BF16), V((6, 3, 9, 16, C), BF16),
             V((6, 20, 8, C), F32), V((6, 3, 5, 8, C), F32), V((6, 4, 5, 8, C), F32),
-            V((4, 4, 8, C), F32),
+            V((4, 4, 8, C), F32), V((2, 8, C), F32),
             V((2, 512, C), F32), V((2, 512, C), F32),
             dma((4,)), dma((2, 8)), dma((2, 8)), dma((6,)), dma((6,)),
             dma((6,)), dma((6,)), dma((6,)), dma((6,)), dma((6,)), dma((6,)),
             dma((6,)), dma((6,)), dma((6,)), dma((6,)),
-            dma((6,)), dma((6,)), dma((10,)), dma((10,)),
+            dma((6,)), dma((6,)), dma((1,)), dma((1,)), dma((10,)), dma((10,)),
         ],
         compiler_params=pltpu.CompilerParams(
             collective_id=0, has_side_effects=True, vmem_limit_bytes=56 * 2**20

time: 52.9 us -> 51.9 us (0.981)
  Pallas kernels: 52 us -> 51.1 us
    pallas_call x1, Pallas kernels: 49.3 us -> 48.5 us  [per_device(): pl.pallas_call(step_kernel, out_shape=(V((2, 2, 512, C), BF16), V((6, 2,...]
where the time goes in v5:
time: 51.9 us; the launch traced here: 51.8 us
  Pallas kernels  51.1 us (98%)
  between operations  0.64 us (1%)
    pallas_call x1, Pallas kernels, per_device(): pl.pallas_call(step_kernel, out_shape=(V((2, 2, 512, C), BF16), V((6, 2,...  48.5 us
    pallas_call x1, Pallas kernels, per_device(): pl.pallas_call(finish_kernel, out_shape=(jax.ShapeDtypeStruct((2, 512, C)...  2.63 us

profile of v5, /device:TPU:1, one launch (start us, length us, event | category | flops | bytes accessed | tf_op | source)
XLA Modules:
  0.0 51.8 jit_solution(4113267499400253287)
XLA Ops:
  0.6 48.5 %step.1 = (bf16[2,2,512,128]{3,2,1,0:T(8,128)(2,1)S(1)}, bf16[6,2,4,20,8,128]{5,4,3,2,1,0:T(8,128)(2,1)S(1)}, f32[2,8,128]{2,1,0:T(8,128)S(1)}) custom-call(s32[2]{0:T(128)} %pos_ref.1, f32[1,128]{1,0:T(1,128)} %bitcast.2, bf16[2,512,128]{2,1,0:T(8,128)(2,1)} %feat_hbm.1, bf16[2,512,128]{2,1,0:T(8,128)(2,1)} %cot_hbm.1, bf16[27,128,128]{2,1,0:T(8,128)(2,1)} %k1_hbm.1, ...), custom_call_target="tpu_custom_call" | custom-call | tf_op jit(solution)/shard_map/step/pallas_call | solution.py:528
  49.1 2.6 %finish.1 = (bf16[2,512,128]{2,1,0:T(8,128)(2,1)}, bf16[2,512,128]{2,1,0:T(8,128)(2,1)}, f32[2,27,128,128]{3,2,1,0:T(8,128)}, f32[1,128]{1,0:T(1,128)}) custom-call(bf16[2,2,512,128]{3,2,1,0:T(8,128)(2,1)S(1)} %get-tuple-element.11.outv, bf16[6,2,4,20,8,128]{5,4,3,2,1,0:T(8,128)(2,1)S(1)} %get-tuple-element.12.full_ref, ...), custom_call_target="tpu_custom_call" | custom-call | tf_op jit(solution)/shard_map/finish/pallas_call | solution.py:556

commit v6 on v5

--- a/solution.py
+++ b/solution.py
@@ -27,7 +27,7 @@
 def step_kernel(
     pos_ref, gain_ref, feat_hbm, cot_hbm, k1_hbm, k2_hbm,
     outv, full_ref, stats_ref,
-    feat, cot, w1, w2, r1, r2, grid1, land, grid2, ag, au, ah, ap, pre_ref, hid_t, pgr_t,
+    feat, cot, w1, w2, r1, r2, r2y, grid1, land, grid2, ag, au, ah, ap, pre_ref, hg_ref, hid_t, pgr_t,
     hid, pgr, part, rcore, sa, ra, sb, rb, rc, gains, sums, units, invs,
     in_sem, hs, hr, cs, cr, a_s, a_r, b_s, b_r, c_s, c_r, eb_s, eb_r, ea_s, ea_r, sib_s, sib_r, sums_s, sums_r, gs, gr,
 ):
@@ -145,6 +145,7 @@
     loads[3].wait()
     for t in range(27):
         r2[t // 9, :, pl.ds(t % 9 * C, C)] = w2[26 - t]
+        r2y[t // 9, t % 9 // 3, :, pl.ds(t % 3 * C, C)] = w2[26 - t]
 
     z = lax.broadcasted_iota(jnp.int32, (10, 8, C), 1)
     first, last = z == 0, z == 7
@@ -218,10 +219,16 @@
             lambda rows, ox, oy: jnp.dot(
                 rows, w1[pl.ds(ox * 9 + oy * 3, 3)].reshape(3 * C, C), preferred_element_type=F32))
 
+    def fix_second(s):
+        fix(au, s, 1, hg_ref.at[s],
+            lambda rows, ox: lax.dot_general(rows, r2[ox], NT, preferred_element_type=F32),
+            lambda rows, ox, oy: lax.dot_general(rows, r2y[ox, oy], NT, preferred_element_type=F32))
+
     def first_local(s, carry):
         gather(ag, s, grid1, 0)
         pre_ref[s] = conv(ag, s, w1).reshape(8, 8, 8, C)
         gather(au, s, grid1, 1)
+        hg_ref[s] = conv_t(au, s, r2).reshape(8, 8, 8, C)
         return carry
 
     lax.fori_loop(0, 2, first_local, 0)
@@ -410,7 +417,8 @@
         return carry
 
     def backward(s, total):
-        hgrad = conv_t(au, s, r2) * pick(live, s)
+        fix_second(s)
+        hgrad = hg_ref[s].reshape(512, C) * pick(live, s)
         unit, inv = units[s], invs[s]
         normed = unit * gain
         sig = jax.nn.sigmoid(normed)
@@ -533,10 +541,10 @@
         scratch_shapes=[
             V((2, 512, C), BF16), V((2, 512, C), BF16),
             V((27, C, C), BF16), V((27, C, C), BF16),
-            V((3, C, 9 * C), BF16), V((3, C, 9 * C), BF16),
+            V((3, C, 9 * C), BF16), V((3, C, 9 * C), BF16), V((3, 3, C, 3 * C), BF16),
             V((2, 18, 18, 8, C), BF16), V((2, 18, 18, 8, C), BF16), V((2, 18, 18, 8, C), BF16),
             V(tile, BF16), V(tile, BF16), V(tile, BF16), V(tile, BF16),
-            V((2, 8, 8, 8, C), F32), V((2, C, 512), BF16), V((2, C, 512), BF16),
+            V((2, 8, 8, 8, C), F32), V((2, 8, 8, 8, C), F32), V((2, C, 512), BF16), V((2, C, 512), BF16),
             V((2, 512, C), BF16), V((2, 512, C), BF16),
             V((54, C, C), F32), V((54, 64, C), F32),
             V((6, 9, 4, 16, C), BF16), V((6, 3, 9, 16, C), BF16),

time: 51.9 us -> 51.2 us (0.987)
  Pallas kernels: 51.1 us -> 50.4 us
    pallas_call x1, Pallas kernels: 48.5 us -> 47.8 us  [per_device(): pl.pallas_call(step_kernel, out_shape=(V((2, 2, 512, C), BF16), V((6, 2,...]
where the time goes in v6:
time: 51.2 us; the launch traced here: 51.1 us
  Pallas kernels  50.4 us (98%)
  between operations  0.64 us (1%)
    pallas_call x1, Pallas kernels, per_device(): pl.pallas_call(step_kernel, out_shape=(V((2, 2, 512, C), BF16), V((6, 2,...  47.8 us
    pallas_call x1, Pallas kernels, per_device(): pl.pallas_call(finish_kernel, out_shape=(jax.ShapeDtypeStruct((2, 512, C)...  2.63 us

profile of v6, /device:TPU:1, one launch (start us, length us, event | category | flops | bytes accessed | tf_op | source)
XLA Modules:
  0.0 51.1 jit_solution(5105471638293358257)
XLA Ops:
  0.6 47.8 %step.1 = (bf16[2,2,512,128]{3,2,1,0:T(8,128)(2,1)S(1)}, bf16[6,2,4,20,8,128]{5,4,3,2,1,0:T(8,128)(2,1)S(1)}, f32[2,8,128]{2,1,0:T(8,128)S(1)}) custom-call(s32[2]{0:T(128)} %pos_ref.1, f32[1,128]{1,0:T(1,128)} %bitcast.2, bf16[2,512,128]{2,1,0:T(8,128)(2,1)} %feat_hbm.1, bf16[2,512,128]{2,1,0:T(8,128)(2,1)} %cot_hbm.1, bf16[27,128,128]{2,1,0:T(8,128)(2,1)} %k1_hbm.1, ...), custom_call_target="tpu_custom_call" | custom-call | tf_op jit(solution)/shard_map/step/pallas_call | solution.py:536
  48.4 2.6 %finish.1 = (bf16[2,512,128]{2,1,0:T(8,128)(2,1)}, bf16[2,512,128]{2,1,0:T(8,128)(2,1)}, f32[2,27,128,128]{3,2,1,0:T(8,128)}, f32[1,128]{1,0:T(1,128)}) custom-call(bf16[2,2,512,128]{3,2,1,0:T(8,128)(2,1)S(1)} %get-tuple-element.11.outv, bf16[6,2,4,20,8,128]{5,4,3,2,1,0:T(8,128)(2,1)S(1)} %get-tuple-element.12.full_ref, ...), custom_call_target="tpu_custom_call" | custom-call | tf_op jit(solution)/shard_map/finish/pallas_call | solution.py:564

commit v7 on v6

--- a/solution.py
+++ b/solution.py
@@ -163,7 +163,7 @@
             return carry
 
         if layers is None:
-            lax.fori_loop(0, 10, layer, 0)
+            lax.fori_loop(0, 10, layer, 0, unroll=2)
         else:
             for x in layers:
                 layer(x, 0)
@@ -178,7 +178,7 @@
                     a[s, x, pl.ds(oy * 24, 16), pl.ds((oy * 3 + oz) * C, C)] = v.reshape(16, C).astype(BF16)
             return carry
 
-        lax.fori_loop(1, 9, layer, 0)
+        lax.fori_loop(1, 9, layer, 0, unroll=4)
 
     def conv(a, s, w):
         total = None

time: 51.2 us -> 50.6 us (0.988)
    pallas_call x1, Pallas kernels: 47.8 us -> 47.2 us  [per_device(): pl.pallas_call(step_kernel, out_shape=(V((2, 2, 512, C), BF16), V((6, 2,...]
where the time goes in v7:
time: 50.6 us; the launch traced here: 50.5 us
  Pallas kernels  49.9 us (99%)
  between operations  0.64 us (1%)
    pallas_call x1, Pallas kernels, per_device(): pl.pallas_call(step_kernel, out_shape=(V((2, 2, 512, C), BF16), V((6, 2,...  47.2 us
    pallas_call x1, Pallas kernels, per_device(): pl.pallas_call(finish_kernel, out_shape=(jax.ShapeDtypeStruct((2, 512, C)...  2.63 us

profile of v7, /device:TPU:1, one launch (start us, length us, event | category | flops | bytes accessed | tf_op | source)
XLA Modules:
  0.0 50.5 jit_solution(13359446861829730236)
XLA Ops:
  0.6 47.2 %step.1 = (bf16[2,2,512,128]{3,2,1,0:T(8,128)(2,1)S(1)}, bf16[6,2,4,20,8,128]{5,4,3,2,1,0:T(8,128)(2,1)S(1)}, f32[2,8,128]{2,1,0:T(8,128)S(1)}) custom-call(s32[2]{0:T(128)} %pos_ref.1, f32[1,128]{1,0:T(1,128)} %bitcast.2, bf16[2,512,128]{2,1,0:T(8,128)(2,1)} %feat_hbm.1, bf16[2,512,128]{2,1,0:T(8,128)(2,1)} %cot_hbm.1, bf16[27,128,128]{2,1,0:T(8,128)(2,1)} %k1_hbm.1, ...), custom_call_target="tpu_custom_call" | custom-call | tf_op jit(solution)/shard_map/step/pallas_call | solution.py:536
  47.9 2.6 %finish.1 = (bf16[2,512,128]{2,1,0:T(8,128)(2,1)}, bf16[2,512,128]{2,1,0:T(8,128)(2,1)}, f32[2,27,128,128]{3,2,1,0:T(8,128)}, f32[1,128]{1,0:T(1,128)}) custom-call(bf16[2,2,512,128]{3,2,1,0:T(8,128)(2,1)S(1)} %get-tuple-element.11.outv, bf16[6,2,4,20,8,128]{5,4,3,2,1,0:T(8,128)(2,1)S(1)} %get-tuple-element.12.full_ref, ...), custom_call_target="tpu_custom_call" | custom-call | tf_op jit(solution)/shard_map/finish/pallas_call | solution.py:564

commit v8 on v7

--- a/solution.py
+++ b/solution.py
@@ -299,7 +299,7 @@
             sa[g, k] = v.reshape(4, 16, C).astype(BF16)
             return carry
 
-        lax.fori_loop(0, 9, tap, 0)
+        lax.fori_loop(0, 9, tap, 0, unroll=3)
         three(axes(g)[0], lambda k, to, d: remote(
             sa.at[g, :, to], ra.at[g, k], a_s.at[g], a_r.at[g], d))
 

time: 50.6 us -> 50.5 us (level)
  no operation moved by 1% of the time
where the time goes in v8:
time: 50.5 us; the launch traced here: 50.4 us
  Pallas kernels  49.8 us (99%)
  between operations  0.64 us (1%)
    pallas_call x1, Pallas kernels, per_device(): pl.pallas_call(step_kernel, out_shape=(V((2, 2, 512, C), BF16), V((6, 2,...  47.1 us
    pallas_call x1, Pallas kernels, per_device(): pl.pallas_call(finish_kernel, out_shape=(jax.ShapeDtypeStruct((2, 512, C)...  2.63 us

profile of v8, /device:TPU:1, one launch (start us, length us, event | category | flops | bytes accessed | tf_op | source)
XLA Modules:
  0.0 50.4 jit_solution(6644062312911796515)
XLA Ops:
  0.6 47.1 %step.1 = (bf16[2,2,512,128]{3,2,1,0:T(8,128)(2,1)S(1)}, bf16[6,2,4,20,8,128]{5,4,3,2,1,0:T(8,128)(2,1)S(1)}, f32[2,8,128]{2,1,0:T(8,128)S(1)}) custom-call(s32[2]{0:T(128)} %pos_ref.1, f32[1,128]{1,0:T(1,128)} %bitcast.2, bf16[2,512,128]{2,1,0:T(8,128)(2,1)} %feat_hbm.1, bf16[2,512,128]{2,1,0:T(8,128)(2,1)} %cot_hbm.1, bf16[27,128,128]{2,1,0:T(8,128)(2,1)} %k1_hbm.1, ...), custom_call_target="tpu_custom_call" | custom-call | tf_op jit(solution)/shard_map/step/pallas_call | solution.py:536
  47.8 2.6 %finish.1 = (bf16[2,512,128]{2,1,0:T(8,128)(2,1)}, bf16[2,512,128]{2,1,0:T(8,128)(2,1)}, f32[2,27,128,128]{3,2,1,0:T(8,128)}, f32[1,128]{1,0:T(1,128)}) custom-call(bf16[2,2,512,128]{3,2,1,0:T(8,128)(2,1)S(1)} %get-tuple-element.11.outv, bf16[6,2,4,20,8,128]{5,4,3,2,1,0:T(8,128)(2,1)S(1)} %get-tuple-element.12.full_ref, ...), custom_call_target="tpu_custom_call" | custom-call | tf_op jit(solution)/shard_map/finish/pallas_call | solution.py:564
